TPU v7x, 32 devices: a whole 2x2x4 slice. The times are simulated.
32 devices in a mesh: neur: 4 (over z), tri: 4 (over y, x), bin: 2 (over core).
Axes of the slice: x: 2, y: 2, z: 4, core: 2. Of those that a mesh axis runs over, the one named last changes fastest.
Arguments:
- tensor: bfloat16 [2048, 128, 256], P('neur', 'tri', 'bin'), may hold values from -3600 to 3600
- bin_factor: bfloat16 [256, 64], P('bin'), may hold values from 0.049804688 to 1
- trial_factor: bfloat16 [128, 64], P('tri'), may hold values from 0.049804688 to 1
Outputs:
- neuron_factor: float32 [2048, 64], P(('neur', 'tri', 'bin'))
- weights: float32 [64], replicated
All inputs are finite; a program needn't handle non-finite values.
Results may differ from a plain program's by a relative error of at most 0.0003.
Values sent between devices are 32-bit elements; how exact they have to be, the bound alone decides.
No kernel may reach another device: no remote copies, remote signals or barrier semaphores. Data moves between devices by JAX's collectives and lax.ppermute only.
A program may use at most 64 MiB of HBM per device.

v0:
```python
import jax
import jax.numpy as jnp
from jax import lax
from jax.sharding import PartitionSpec as P


def solve_rows(products, lower):
    return jax.scipy.linalg.cho_solve((lower, True), products.T).T


def local(tensor, bin_factor, trial_factor):
    rows, trials, bins = tensor.shape
    rank = bin_factor.shape[1]
    bin_part = jnp.dot(bin_factor.T, bin_factor, preferred_element_type=jnp.float32)
    trial_part = jnp.dot(trial_factor.T, trial_factor, preferred_element_type=jnp.float32)
    bin_gram = lax.psum(bin_part, "bin")
    trial_gram = lax.psum(trial_part, "tri")
    lower = jnp.linalg.cholesky(bin_gram * trial_gram)
    section = jnp.dot(
        tensor.reshape(rows * trials, bins), bin_factor, preferred_element_type=jnp.float32
    )
    section = section.reshape(rows, trials, rank)
    partial_value = jnp.sum(section * trial_factor.astype(jnp.float32)[None], axis=1)
    neurons_all = rows * lax.axis_size("neur")
    block = lax.psum(partial_value, ("tri", "bin"))
    block_solved = solve_rows(block, lower)
    squares = lax.psum(jnp.sum(block_solved * block_solved, axis=0), "neur")
    share = rows // (lax.axis_size("tri") * lax.axis_size("bin"))
    offset = (lax.axis_index("tri") * lax.axis_size("bin") + lax.axis_index("bin")) * share
    solved = lax.dynamic_slice_in_dim(block_solved, offset, share, 0)
    weights = jnp.sqrt(squares / neurons_all + 1e-06)
    return (solved / weights, weights)


def solution(mesh):
    return jax.shard_map(
        local,
        mesh=mesh,
        in_specs=(P("neur", "tri", "bin"), P("bin", None), P("tri", None)),
        out_specs=(P(("neur", "tri", "bin"), None), P()),
        check_vma=False,
    )
```

profile of v0, /device:TPU:0, one launch (start us, length us, event | category | flops | bytes accessed | tf_op | source)
XLA Modules:
  0.0 92.7 jit_solution(17252243305932020055)
XLA Ops:
  7.2 0.0 copy-start
  7.2 0.0 copy-start.1
  7.2 0.0 all-reduce.2.cloned.1.call-start
  7.2 0.7 convert_element_type.3
  8.0 0.0 copy-done
  8.0 7.6 %multiply_reduce_fusion = f32[512,64]{0,1:T(8,128)} fusion(bf16[512,32,128]{2,1,0:T(8,128)(2,1)} %param.3, f32[32,64]{1,0:T(8,128)S(1)} %convert_element_type.3, bf16[128,64]{0,1:T(8,128)(2,1)S(1)} %copy-done), kind=kOutput, calls=%fused_computation.2 | convolution fusion | flops 270499840 | bytes 4349952 | tf_op jit(solution)/shard_map/dot_general | solution.py:19
  15.5 0.0 all-reduce.2.cloned.1.call-update
  15.5 0.1 fusion.11
  15.7 0.0 copy-done.1
  15.7 0.2 fusion.12
  15.9 3.7 %psum.28 = f32[64,64]{0,1:T(8,128)S(1)} all-reduce(f32[64,64]{0,1:T(8,128)S(1)} %fusion.11), channel_id=1, replica_groups=mesh['neur'=4,'tri'=4,'bin'=2] {'bin'}, use_global_device_ids=true, to_apply=%region_0.0 | all-reduce | flops 4096 | bytes 32768 | tf_op jit(solution)/shard_map/psum | solution.py:16
  19.6 17.5 %psum.29 = f32[64,64]{0,1:T(8,128)S(1)} all-reduce(f32[64,64]{0,1:T(8,128)S(1)} %fusion.12), channel_id=1, replica_groups=mesh['neur'=4,'tri'=4,'bin'=2] {'tri'}, use_global_device_ids=true, to_apply=%region_1.0 | all-reduce | flops 4096 | bytes 32768 | tf_op jit(solution)/shard_map/psum | solution.py:17
  37.1 0.1 copy.11
  37.1 5.9 %cholesky.16 = f32[64,64]{1,0:T(8,128)S(1)} custom-call(f32[64,64]{1,0:T(8,128)S(1)} %fusion.9), custom_call_target="Cholesky" | custom-call | tf_op jit(solution)/shard_map/jit(cholesky)/cholesky | solution.py:18
  43.0 0.6 compare_reduce_fusion
  43.7 0.7 fusion.4
  44.3 4.9 %custom-call.10 = f32[1,64,64]{1,2,0:T(8,128)S(1)} custom-call(f32[1,64,64]{2,1,0:T(8,128)S(1)} %fusion.4), custom_call_target="InvertDiagBlocksLowerTriangular" | custom-call | tf_op jit(solution)/shard_map/jit(_cho_solve)/triangular_solve | solution.py:8
  49.2 22.5 %all-reduce.2.cloned.1.call-done = f32[512,64]{0,1:T(8,128)} async-done(((f32[512,64]{0,1:T(8,128)}), f32[512,64]{0,1:T(8,128)}) %all-reduce.2.cloned.1.call-update) | async-done | bytes 131088 | tf_op jit(solution)/shard_map/psum | solution.py:25
  71.8 1.2 %fusion.7 = f32[64,512]{1,0:T(8,128)S(1)} fusion(f32[512,64]{0,1:T(8,128)} %all-reduce.2.cloned.1.call-done, f32[1,64,64]{1,2,0:T(8,128)S(1)} %custom-call.10), kind=kOutput, calls=%fused_computation.8 | convolution fusion | flops 25165824 | bytes 278528 | tf_op jit(solution)/shard_map/jit(_cho_solve)/triangular_solve | solution.py:8
  73.0 0.4 multiply_reduce_fusion.1
  73.4 11.7 %psum.31 = f32[64]{0:T(128)S(1)} all-reduce(f32[64]{0:T(128)S(1)} %get-tuple-element.6), channel_id=1, replica_groups=mesh['neur'=4,'tri'=4,'bin'=2] {'neur'}, use_global_device_ids=true, to_apply=%region_7.8 | all-reduce | flops 64 | bytes 512 | tf_op jit(solution)/shard_map/psum | solution.py:27
  85.1 0.0 copy-start.2
  85.1 0.1 dynamic-slice_divide_fusion
  85.2 0.7 copy.12
  85.9 0.0 copy-done.2
  (4 shorter events, 0.1 us)
Async XLA Ops:
  7.2 0.8 copy-start
  7.2 8.5 %copy-start.1 = (bf16[32,64]{1,0:T(8,128)(2,1)S(1)}, bf16[32,64]{1,0:T(8,128)(2,1)}, u32[]{:S(2)}) copy-start(bf16[32,64]{1,0:T(8,128)(2,1)} %param.5) | copy-start | bytes 12292
  7.2 64.6 %all-reduce.2.cloned.1.call-start = ((), (), s32[]{:S(2)}) async-start(), calls=%async_computation | async-start | bytes 262144 | tf_op jit(solution)/shard_map/psum | solution.py:25
  85.1 0.8 copy-start.2
Sparse Core Ops, SparseCore 0:
  15.7 56.0 all-reduce.1
where the time goes:
time: 93.1 us; the launch traced here: 92.7 us
  blocking collectives  32.8 us (35%)
  waiting for transfers between devices  22.6 us (24%)
  between operations  14.1 us (15%)
  other arithmetic  12.9 us (14%)
  matrix products  9.46 us (10%)
    psum x1, waiting for transfers between devices, local(): block = lax.psum(partial_value, ('tri', 'bin'))  22.5 us
    psum x1, blocking collectives, local(): trial_gram = lax.psum(trial_part, 'tri')  17.5 us
    psum x1, blocking collectives, local(): squares = lax.psum(jnp.sum(block_solved * block_solved, axis=0), 'neur')  11.7 us
    dot_general x1, matrix products, local(): jnp.dot(tensor.reshape(rows * trials, bins), bin_factor, preferred_elemen...  7.56 us
    another operation x3, other arithmetic, local(): lower = jnp.linalg.cholesky(bin_gram * trial_gram)  6.53 us
    another operation x2, other arithmetic, solve_rows(): return jax.scipy.linalg.cho_solve((lower, True), products.T).T  5.55 us
    psum x1, blocking collectives, local(): bin_gram = lax.psum(bin_part, 'bin')  3.68 us
  transfers between devices with their start and end apart: 1, of which 1 were waited for; matrix products, arithmetic and copies ran while one was open for 13% of the time, Pallas kernels for 0%

commit v1 on v0

v1 whole, which is shorter than its diff:
```python
import functools

import jax
import jax.numpy as jnp
from jax import lax
from jax.experimental import pallas as pl
from jax.experimental.pallas import tpu as pltpu
from jax.sharding import PartitionSpec as P

SUB = 8
EXACT = lax.Precision.HIGHEST


def parity(index, count):
    result = index & 1
    for bit in range(1, count.bit_length() - 1):
        result = result ^ ((index >> bit) & 1)
    return result


def gram_of(factor_t):
    return lax.dot_general(factor_t, factor_t, (((1,), (1,)), ((), ())), preferred_element_type=jnp.float32)


def product_kernel(send_gram, half_ref, tensor_ref, bin_t_ref, trial_ref, out_ref, wide_ref):
    step = pl.program_id(0)
    rows, trials, bins = tensor_ref.shape
    rank = bin_t_ref.shape[0]
    pair = trials // 2

    @pl.when(step == 0)
    def _():
        bin_t = bin_t_ref[...]
        zero = jnp.zeros_like(bin_t)
        wide_ref[:rank, :bins] = bin_t
        wide_ref[:rank, bins:] = zero
        wide_ref[rank:, :bins] = zero
        wide_ref[rank:, bins:] = bin_t
        top = rows * pl.num_programs(0)
        if send_gram:
            out_ref[pl.ds(top, rank), :] = gram_of(bin_t)
        else:
            trial = trial_ref[...]
            out_ref[pl.ds(top, rank), :] = lax.dot_general(trial, trial, (((0,), (0,)), ((), ())), preferred_element_type=jnp.float32)

    trial = trial_ref[...].astype(jnp.float32)
    trial = jnp.concatenate([trial[:pair], trial[pair:]], axis=1)
    low = tensor_ref[:, :pair, :].reshape(rows * pair, bins)
    high = tensor_ref[:, pair:, :].reshape(rows * pair, bins)
    section = lax.dot_general(
        jnp.concatenate([low, high], axis=1), wide_ref[...], (((1,), (1,)), ((), ())), preferred_element_type=jnp.float32
    )
    total = jnp.sum(section.reshape(rows, pair, 2 * rank) * trial[None], axis=1)
    out_ref[pl.ds(pl.multiple_of(step * rows, SUB), rows), :] = total[:, :rank] + total[:, rank:]


def products(tensor, bin_t, trial_factor, half, steps, send_gram):
    neurons, trials, bins = tensor.shape
    rank = bin_t.shape[0]
    rows = neurons // (2 * steps)
    return pl.pallas_call(
        functools.partial(product_kernel, send_gram),
        grid_spec=pltpu.PrefetchScalarGridSpec(
            num_scalar_prefetch=1,
            grid=(steps,),
            in_specs=[
                pl.BlockSpec((rows, trials, bins), lambda t, half: (2 * t + (half[0] ^ parity(t, steps)), 0, 0)),
                pl.BlockSpec((rank, bins), lambda t, half: (0, 0)),
                pl.BlockSpec((trials, rank), lambda t, half: (0, 0)),
            ],
            out_specs=pl.BlockSpec((rows * steps + rank, rank), lambda t, half: (0, 0)),
            scratch_shapes=[pltpu.VMEM((2 * rank, 2 * bins), jnp.bfloat16)],
        ),
        out_shape=jax.ShapeDtypeStruct((rows * steps + rank, rank), jnp.float32),
        name="products",
    )(half, tensor, bin_t, trial_factor)


def inverse_tiles(tiles):
    shape = tiles[0].shape
    count = len(tiles)
    lane = lax.broadcasted_iota(jnp.int32, shape, 1)
    sub = lax.broadcasted_iota(jnp.int32, shape, 0)
    across = lambda tile, j: jnp.broadcast_to(tile[:, j : j + 1], shape)
    down = lambda tile, i: jnp.broadcast_to(tile[i : i + 1, :], shape)
    for panel in range(count):
        base = panel * SUB
        columns = [across(tiles[panel], base + j) for j in range(SUB)]
        block = tiles[panel]
        for k in range(SUB):
            scale = 1.0 / down(columns[k], k)
            column = columns[k]
            row = jnp.where(lane == base + k, 1.0, down(block, k)) * scale
            block = jnp.where(sub == k, row, jnp.where(lane == base + k, 0.0, block) - column * row)
            for j in range(k + 1, SUB):
                row = down(columns[j], k) * scale
                columns[j] = jnp.where(sub == k, row, columns[j] - column * row)
        inside = (lane >= base) & (lane < base + SUB)
        rows = [down(block, j) for j in range(SUB)]
        updated = {panel: block}
        for index in range(1, count):
            index = (panel + index) % count
            tile = tiles[index]
            even = across(tile, base) * rows[0]
            odd = jnp.where(inside, 0.0, tile)
            for j in range(1, SUB):
                if j % 2:
                    odd = odd - across(tile, base + j) * rows[j]
                else:
                    even = even + across(tile, base + j) * rows[j]
            updated[index] = odd - even
        tiles = [updated[index] for index in range(count)]
    return tiles


def inverse_kernel(bin_a_ref, bin_b_ref, trial_a_ref, trial_b_ref, out_ref):
    rank = out_ref.shape[0]
    gram = (bin_a_ref[...] + bin_b_ref[...]) * (trial_a_ref[...] + trial_b_ref[...])
    tiles = [gram[i : i + SUB, :] for i in range(0, rank, SUB)]
    for i, tile in enumerate(inverse_tiles(tiles)):
        out_ref[i * SUB : (i + 1) * SUB, :] = tile


def solve_kernel(own_ref, other_ref, inverse_ref, solved_ref, squares_ref):
    solved = jnp.dot(own_ref[...] + other_ref[...], inverse_ref[...], preferred_element_type=jnp.float32, precision=EXACT)
    solved_ref[...] = solved
    squares_ref[...] = jnp.broadcast_to(jnp.sum(solved * solved, axis=0, keepdims=True), squares_ref.shape)


def local(neur, tri, tensor, bin_factor, trial_factor):
    axes = ("neur", "tri", "bin")
    rank = bin_factor.shape[1]

    def swap(value, n, t, b):
        flat = lambda i, j, k: (i * tri + j) * 2 + k
        pairs = [(flat(i, j, k), flat(i ^ n, j ^ t, k ^ b)) for i in range(neur) for j in range(tri) for k in range(2)]
        return lax.ppermute(value, axes, pairs)

    rows = tensor.shape[0]
    share = rows // (2 * tri)
    place = lax.axis_index("tri")
    half = (lax.axis_index("bin") ^ parity(place, tri)).astype(jnp.int32)
    bin_t = bin_factor.T
    sent = products(tensor, bin_t, trial_factor, (1 - half)[None], tri, True)
    got = swap(sent, 0, 0, 1)
    own = products(tensor, bin_t, trial_factor, half[None], tri, False)
    bin_a, bin_b = sent[share * tri :], got[share * tri :]
    block = own[: share * tri] + got[: share * tri]
    trial_gram = own[share * tri :]
    bit = 1
    while bit < tri // 2:
        joined = jnp.concatenate([block, trial_gram], axis=0)
        joined = joined + swap(joined, 0, bit, 1)
        block, trial_gram = joined[: share * tri], joined[share * tri :]
        bit *= 2
    trial_other = swap(trial_gram, 0, bit, 1)
    trial_gram, block = lax.optimization_barrier((trial_gram, block))
    other = swap(block, 0, bit, 1)
    f32 = jnp.float32
    inverse = pl.pallas_call(inverse_kernel, out_shape=jax.ShapeDtypeStruct((rank, rank), f32), name="inverse")(
        bin_a, bin_b, trial_gram, trial_other
    )
    solved, squares = pl.pallas_call(
        solve_kernel,
        out_shape=(jax.ShapeDtypeStruct((share * tri, rank), f32), jax.ShapeDtypeStruct((SUB, rank), f32)),
        name="solve",
    )(block, other, inverse)
    squares = squares + swap(squares, 0, 0, 1)
    bit = 1
    while bit < neur:
        if bit * 2 < neur:
            one, two, three = (swap(squares, k * bit, 0, 1) for k in (1, 2, 3))
            squares = (squares + one) + (two + three)
            bit *= 4
        else:
            squares = squares + swap(squares, bit, 0, 1)
            bit *= 2
    weights = jnp.sqrt(squares[0] / (rows * neur) + 1e-06)
    mine = lax.dynamic_slice_in_dim(solved, place * share, share, 0)
    return (mine / weights, weights)


def solution(mesh):
    return jax.shard_map(
        functools.partial(local, mesh.shape["neur"], mesh.shape["tri"]),
        mesh=mesh,
        in_specs=(P("neur", "tri", "bin"), P("bin", None), P("tri", None)),
        out_specs=(P(("neur", "tri", "bin"), None), P()),
        check_vma=False,
    )
```

time: 93.1 us -> 41.8 us (0.45)
  blocking collectives: 32.8 us -> 0 us
  between operations: 14.1 us -> 0.72 us
  Pallas kernels: 0 us -> 13.2 us
  waiting for transfers between devices: 22.6 us -> 11.3 us
  other arithmetic: 12.9 us -> 3.05 us
  matrix products: 9.46 us -> 0 us
  starting transfers between devices: 0.04 us -> 8.96 us
  local copies, waits for them, and re-layouts: 0.79 us -> 4.02 us
    psum x3 -> x0, blocking collectives: 32.8 us -> none  [the longest x1 17.5 us: local(): trial_gram = lax.psum(trial_part, 'tri')]
    psum x1 -> x0, waiting for transfers between devices: 22.5 us -> none  [local(): block = lax.psum(partial_value, ('tri', 'bin'))]
    pallas_call x0 -> x4, Pallas kernels: none -> 13.2 us  [the longest x2 8.26 us: products(): pl.pallas_call(functools.partial(product_kernel, send_gram), grid_spec=pl...]
    another operation x5 -> x0, other arithmetic: 12.1 us -> none  [the longest x3 6.53 us: local(): lower = jnp.linalg.cholesky(bin_gram * trial_gram)]
    ppermute x0 -> x8, waiting for transfers between devices: none -> 11.3 us  [swap(): return lax.ppermute(value, axes, pairs)]
    ppermute x0 -> x8, starting transfers between devices: none -> 8.96 us  [swap(): return lax.ppermute(value, axes, pairs)]
    dot_general x3 -> x0, matrix products: 7.89 us -> none  [the longest x1 7.56 us: local(): jnp.dot(tensor.reshape(rows * trials, bins), bin_factor, preferred_elemen...]
    slice x0 -> x5, local copies, waits for them, and re-layouts: none -> 2.76 us  [the longest x2 1.98 us: local(): bin_a, bin_b = (sent[share * tri:], got[share * tri:])]
  transfers between devices with their start and end apart: 1 -> 8, of which waited for: 1 -> 5; matrix products, arithmetic and copies ran while one was open for 13% -> 7% of each run, Pallas kernels for 0% -> 17%
where the time goes in v1:
time: 41.8 us; the launch traced here: 41.2 us
  Pallas kernels  13.2 us (32%)
  waiting for transfers between devices  11.3 us (27%)
  starting transfers between devices  8.96 us (21%)
  local copies, waits for them, and re-layouts  4.02 us (10%)
  other arithmetic  3.05 us (7%)
  between operations  0.72 us (2%)
    ppermute x8, waiting for transfers between devices, swap(): return lax.ppermute(value, axes, pairs)  11.3 us
    ppermute x8, starting transfers between devices, swap(): return lax.ppermute(value, axes, pairs)  8.96 us
    pallas_call x2, Pallas kernels, products(): pl.pallas_call(functools.partial(product_kernel, send_gram), grid_spec=pl...  8.26 us
    pallas_call x1, Pallas kernels, local(): pl.pallas_call(inverse_kernel, out_shape=jax.ShapeDtypeStruct((rank, rank...  3.03 us
    slice x2, local copies, waits for them, and re-layouts, local(): bin_a, bin_b = (sent[share * tri:], got[share * tri:])  1.98 us
    pallas_call x1, Pallas kernels, local(): pl.pallas_call(solve_kernel, out_shape=(jax.ShapeDtypeStruct((share * tri...  1.87 us
    div x2, other arithmetic, local(): return (mine / weights, weights)  1.4 us
    unnamed x10, local copies, waits for them, and re-layouts  1.26 us
  transfers between devices with their start and end apart: 8, of which 5 were waited for; matrix products, arithmetic and copies ran while one was open for 7% of the time, Pallas kernels for 17%

profile of v1, /device:TPU:0, one launch (start us, length us, event | category | flops | bytes accessed | tf_op | source)
XLA Modules:
  0.0 41.2 jit_solution(6714373346555918371)
XLA Ops:
  0.6 4.1 %products.3 = f32[320,64]{1,0:T(8,128)} custom-call(s32[1]{0:T(128)} %bitcast.2.half_ref, bf16[512,32,128]{2,1,0:T(8,128)(2,1)} %tensor_ref.3, bf16[64,128]{1,0:T(8,128)(2,1)} %bitcast.5, bf16[32,64]{1,0:T(8,128)(2,1)} %trial_ref.3), custom_call_target="tpu_custom_call" | custom-call | tf_op jit(solution)/shard_map/products/pallas_call | solution.py:61
  4.8 0.5 %collective-permute-start = (f32[320,64]{1,0:T(8,128)}, f32[320,64]{1,0:T(8,128)S(1)}, u32[]{:S(2)}, u32[]{:S(2)}) collective-permute-start(f32[320,64]{1,0:T(8,128)} %products.3), channel_id=1, source_target_pairs={{0,1},{1,0},{2,3},{3,2},{4,5},{5,4},{6,7},{7,6},{8,9},{9,8},{10,11... | collective-permute-start | bytes 245768 | tf_op jit(solution)/shard_map/ppermute | solution.py:137
  5.2 4.1 %products.2 = f32[320,64]{1,0:T(8,128)} custom-call(s32[1]{0:T(128)} %bitcast.half_ref, bf16[512,32,128]{2,1,0:T(8,128)(2,1)} %tensor_ref.3, bf16[64,128]{1,0:T(8,128)(2,1)} %bitcast.6, bf16[32,64]{1,0:T(8,128)(2,1)} %trial_ref.3), custom_call_target="tpu_custom_call" | custom-call | tf_op jit(solution)/shard_map/products/pallas_call | solution.py:61
  9.4 0.8 %slice.34 = f32[64,64]{1,0:T(8,128)S(1)} slice(f32[320,64]{1,0:T(8,128)} %products.2), slice={[256:320], [0:64]} | slice | bytes 32768 | tf_op jit(solution)/shard_map/slice | solution.py:149
  10.1 0.0 collective-permute-done
  10.1 0.9 %slice_add_fusion = f32[256,64]{1,0:T(8,128)S(1)} fusion(f32[320,64]{1,0:T(8,128)S(1)} %collective-permute-done, f32[320,64]{1,0:T(8,128)} %products.2), kind=kLoop, calls=%fused_computation.1 | loop fusion | flops 16384 | bytes 196608 | tf_op jit(solution)/shard_map/add | solution.py:148
  11.1 2.7 %collective-permute-start.1 = (f32[320,64]{1,0:T(8,128)S(1)}, f32[320,64]{1,0:T(8,128)S(1)}, u32[]{:S(2)}, u32[]{:S(2)}) collective-permute-start(f32[320,64]{1,0:T(8,128)S(1)} %pad_maximum_fusion), channel_id=1, source_target_pairs={{0,3},{1,2},{2,1},{3,0},{4,7},{5,6},{6,5},{7,4},{8,11},{9,10},{10,... | collective-permute-start | bytes 245768 | tf_op jit(solution)/shard_map/ppermute | solution.py:137
  13.7 4.6 %collective-permute-done.1 = f32[320,64]{1,0:T(8,128)S(1)} collective-permute-done((f32[320,64]{1,0:T(8,128)S(1)}, f32[320,64]{1,0:T(8,128)S(1)}, u32[]{:S(2)}, u32[]{:S(2)}) %collective-permute-start.1) | collective-permute-done | bytes 81952 | tf_op jit(solution)/shard_map/ppermute | solution.py:137
  18.3 0.0 copy-start.1
  18.4 0.0 copy-start
  18.4 1.3 %collective-permute-start.2 = (f32[256,64]{1,0:T(8,128)S(1)}, f32[256,64]{1,0:T(8,128)S(1)}, u32[]{:S(2)}, u32[]{:S(2)}) collective-permute-start(f32[256,64]{1,0:T(8,128)S(1)} %slice.36.own_ref), channel_id=1, source_target_pairs={{0,5},{1,4},{2,7},{3,6},{4,1},{5,0},{6,3},{7,2},{8,13},{9,12},{10,... | collective-permute-start | bytes 196616 | tf_op jit(solution)/shard_map/ppermute | solution.py:137
  19.7 0.5 %collective-permute-start.3 = (f32[64,64]{1,0:T(8,128)S(1)}, f32[64,64]{1,0:T(8,128)S(1)}, u32[]{:S(2)}, u32[]{:S(2)}) collective-permute-start(f32[64,64]{1,0:T(8,128)S(1)} %slice.35.trial_a_ref), channel_id=1, source_target_pairs={{0,5},{1,4},{2,7},{3,6},{4,1},{5,0},{6,3},{7,2},{8,13},{9,12},{10,... | collective-permute-start | bytes 49160 | tf_op jit(solution)/shard_map/ppermute | solution.py:137
  20.2 1.4 %slice.37.bin_a_ref = f32[64,64]{1,0:T(8,128)} slice(f32[320,64]{1,0:T(8,128)} %products.3), slice={[256:320], [0:64]} | slice | bytes 32768 | tf_op jit(solution)/shard_map/slice | solution.py:147
  21.6 0.6 %slice.38.bin_b_ref = f32[64,64]{1,0:T(8,128)} slice(f32[320,64]{1,0:T(8,128)S(1)} %collective-permute-done), slice={[256:320], [0:64]} | slice | bytes 32768 | tf_op jit(solution)/shard_map/slice | solution.py:147
  22.2 2.4 %collective-permute-done.3.trial_b_ref = f32[64,64]{1,0:T(8,128)S(1)} collective-permute-done((f32[64,64]{1,0:T(8,128)S(1)}, f32[64,64]{1,0:T(8,128)S(1)}, u32[]{:S(2)}, u32[]{:S(2)}) %collective-permute-start.3) | collective-permute-done | bytes 16416 | tf_op jit(solution)/shard_map/ppermute | solution.py:137
  24.6 0.0 copy-done.1
  24.6 0.6 %copy-done.3 = f32[64,64]{1,0:T(8,128)} copy-done((f32[64,64]{1,0:T(8,128)}, f32[64,64]{1,0:T(8,128)S(1)}, u32[]{:S(2)}) %copy-start.3) | copy-done | bytes 16408
  25.2 3.0 %inverse.1.inverse_ref = f32[64,64]{1,0:T(8,128)} custom-call(f32[64,64]{1,0:T(8,128)} %slice.37.bin_a_ref, f32[64,64]{1,0:T(8,128)} %slice.38.bin_b_ref, f32[64,64]{1,0:T(8,128)} %copy-done.1, f32[64,64]{1,0:T(8,128)} %copy-done.3), custom_call_target="tpu_custom_call" | custom-call | tf_op jit(solution)/shard_map/inverse/pallas_call | solution.py:160
  28.3 0.0 collective-permute-done.2.other_ref
  28.3 0.6 %copy-done.2 = f32[256,64]{1,0:T(8,128)} copy-done((f32[256,64]{1,0:T(8,128)}, f32[256,64]{1,0:T(8,128)S(1)}, u32[]{:S(2)}) %copy-start.2) | copy-done | bytes 65560
  28.9 1.9 %solve.1 = (f32[256,64]{1,0:T(8,128)}, f32[8,64]{1,0:T(8,128)}) custom-call(f32[256,64]{1,0:T(8,128)} %copy-done, f32[256,64]{1,0:T(8,128)} %copy-done.2, f32[64,64]{1,0:T(8,128)} %inverse.1.inverse_ref), custom_call_target="tpu_custom_call" | custom-call | tf_op jit(solution)/shard_map/solve/pallas_call | solution.py:163
  30.8 0.1 collective-permute-start.4
  30.9 1.3 %collective-permute-done.4 = f32[8,64]{1,0:T(8,128)S(1)} collective-permute-done((f32[8,64]{1,0:T(8,128)}, f32[8,64]{1,0:T(8,128)S(1)}, u32[]{:S(2)}, u32[]{:S(2)}) %collective-permute-start.4) | collective-permute-done | bytes 2080 | tf_op jit(solution)/shard_map/ppermute | solution.py:137
  32.2 0.7 %add.32 = f32[8,64]{1,0:T(8,128)S(1)} add(f32[8,64]{1,0:T(8,128)} %get-tuple-element.9, f32[8,64]{1,0:T(8,128)S(1)} %collective-permute-done.4) | non-fusion elementwise | flops 512 | bytes 6144 | tf_op jit(solution)/shard_map/add | solution.py:168
  32.9 3.0 %collective-permute-start.7 = (f32[8,64]{1,0:T(8,128)S(1)}, f32[8,64]{1,0:T(8,128)S(1)}, u32[]{:S(2)}, u32[]{:S(2)}) collective-permute-start(f32[8,64]{1,0:T(8,128)S(1)} %add.32), channel_id=1, source_target_pairs={{0,25},{1,24},{2,27},{3,26},{4,29},{5,28},{6,31},{7,30},{8,17},{9,... | collective-permute-start | bytes 6152 | tf_op jit(solution)/shard_map/ppermute | solution.py:137
  35.9 0.0 collective-permute-start.6
  35.9 0.9 %collective-permute-start.5 = (f32[8,64]{1,0:T(8,128)S(1)}, f32[8,64]{1,0:T(8,128)S(1)}, u32[]{:S(2)}, u32[]{:S(2)}) collective-permute-start(f32[8,64]{1,0:T(8,128)S(1)} %add.32), channel_id=1, source_target_pairs={{0,9},{1,8},{2,11},{3,10},{4,13},{5,12},{6,15},{7,14},{8,1},{9,0},... | collective-permute-start | bytes 6152 | tf_op jit(solution)/shard_map/ppermute | solution.py:137
  36.8 0.9 %collective-permute-done.7 = f32[8,64]{1,0:T(8,128)S(1)} collective-permute-done((f32[8,64]{1,0:T(8,128)S(1)}, f32[8,64]{1,0:T(8,128)S(1)}, u32[]{:S(2)}, u32[]{:S(2)}) %collective-permute-start.7) | collective-permute-done | bytes 2080 | tf_op jit(solution)/shard_map/ppermute | solution.py:137
  37.7 2.1 %collective-permute-done.6 = f32[8,64]{1,0:T(8,128)S(1)} collective-permute-done((f32[8,64]{1,0:T(8,128)S(1)}, f32[8,64]{1,0:T(8,128)S(1)}, u32[]{:S(2)}, u32[]{:S(2)}) %collective-permute-start.6) | collective-permute-done | bytes 2080 | tf_op jit(solution)/shard_map/ppermute | solution.py:137
  39.8 0.0 collective-permute-done.5
  39.8 0.0 copy-start.4
  39.9 1.4 %dynamic-slice_divide_fusion = f32[64,64]{1,0:T(8,128)} fusion(f32[256,64]{1,0:T(8,128)} %get-tuple-element.8, s32[]{:T(128)S(6)} %select_n.3, f32[64]{0:T(128)S(1)} %sqrt_bitcast_fusion), kind=kLoop, calls=%fused_computation.2 | loop fusion | flops 4096 | bytes 33028 | tf_op jit(solution)/shard_map/div | solution.py:180
  (10 shorter events, 0.1 us)
Async XLA Ops:
  4.8 5.4 %collective-permute-start = (f32[320,64]{1,0:T(8,128)}, f32[320,64]{1,0:T(8,128)S(1)}, u32[]{:S(2)}, u32[]{:S(2)}) collective-permute-start(f32[320,64]{1,0:T(8,128)} %products.3), channel_id=1, source_target_pairs={{0,1},{1,0},{2,3},{3,2},{4,5},{5,4},{6,7},{7,6},{8,9},{9,8},{10,11... | collective-permute-start | bytes 245768 | tf_op jit(solution)/shard_map/ppermute | solution.py:137
  11.1 7.2 %collective-permute-start.1 = (f32[320,64]{1,0:T(8,128)S(1)}, f32[320,64]{1,0:T(8,128)S(1)}, u32[]{:S(2)}, u32[]{:S(2)}) collective-permute-start(f32[320,64]{1,0:T(8,128)S(1)} %pad_maximum_fusion), channel_id=1, source_target_pairs={{0,3},{1,2},{2,1},{3,0},{4,7},{5,6},{6,5},{7,4},{8,11},{9,10},{10,... | collective-permute-start | bytes 245768 | tf_op jit(solution)/shard_map/ppermute | solution.py:137
  18.3 6.3 %copy-start.1 = (f32[64,64]{1,0:T(8,128)}, f32[64,64]{1,0:T(8,128)S(1)}, u32[]{:S(2)}) copy-start(f32[64,64]{1,0:T(8,128)S(1)} %slice.35.trial_a_ref) | copy-start | bytes 49156
  18.4 9.9 %copy-start = (f32[256,64]{1,0:T(8,128)}, f32[256,64]{1,0:T(8,128)S(1)}, u32[]{:S(2)}) copy-start(f32[256,64]{1,0:T(8,128)S(1)} %slice.36.own_ref) | copy-start | bytes 196612
  18.4 9.9 %collective-permute-start.2 = (f32[256,64]{1,0:T(8,128)S(1)}, f32[256,64]{1,0:T(8,128)S(1)}, u32[]{:S(2)}, u32[]{:S(2)}) collective-permute-start(f32[256,64]{1,0:T(8,128)S(1)} %slice.36.own_ref), channel_id=1, source_target_pairs={{0,5},{1,4},{2,7},{3,6},{4,1},{5,0},{6,3},{7,2},{8,13},{9,12},{10,... | collective-permute-start | bytes 196616 | tf_op jit(solution)/shard_map/ppermute | solution.py:137
  19.7 4.9 %collective-permute-start.3 = (f32[64,64]{1,0:T(8,128)S(1)}, f32[64,64]{1,0:T(8,128)S(1)}, u32[]{:S(2)}, u32[]{:S(2)}) collective-permute-start(f32[64,64]{1,0:T(8,128)S(1)} %slice.35.trial_a_ref), channel_id=1, source_target_pairs={{0,5},{1,4},{2,7},{3,6},{4,1},{5,0},{6,3},{7,2},{8,13},{9,12},{10,... | collective-permute-start | bytes 49160 | tf_op jit(solution)/shard_map/ppermute | solution.py:137
  24.6 0.6 %copy-start.3 = (f32[64,64]{1,0:T(8,128)}, f32[64,64]{1,0:T(8,128)S(1)}, u32[]{:S(2)}) copy-start(f32[64,64]{1,0:T(8,128)S(1)} %collective-permute-done.3.trial_b_ref) | copy-start | bytes 49156
  28.3 0.7 %copy-start.2 = (f32[256,64]{1,0:T(8,128)}, f32[256,64]{1,0:T(8,128)S(1)}, u32[]{:S(2)}) copy-start(f32[256,64]{1,0:T(8,128)S(1)} %collective-permute-done.2.other_ref) | copy-start | bytes 196612
  30.8 1.4 %collective-permute-start.4 = (f32[8,64]{1,0:T(8,128)}, f32[8,64]{1,0:T(8,128)S(1)}, u32[]{:S(2)}, u32[]{:S(2)}) collective-permute-start(f32[8,64]{1,0:T(8,128)} %get-tuple-element.9), channel_id=1, source_target_pairs={{0,1},{1,0},{2,3},{3,2},{4,5},{5,4},{6,7},{7,6},{8,9},{9,8},{10,11... | collective-permute-start | bytes 6152 | tf_op jit(solution)/shard_map/ppermute | solution.py:137
  32.9 4.8 %collective-permute-start.7 = (f32[8,64]{1,0:T(8,128)S(1)}, f32[8,64]{1,0:T(8,128)S(1)}, u32[]{:S(2)}, u32[]{:S(2)}) collective-permute-start(f32[8,64]{1,0:T(8,128)S(1)} %add.32), channel_id=1, source_target_pairs={{0,25},{1,24},{2,27},{3,26},{4,29},{5,28},{6,31},{7,30},{8,17},{9,... | collective-permute-start | bytes 6152 | tf_op jit(solution)/shard_map/ppermute | solution.py:137
  35.9 3.9 %collective-permute-start.6 = (f32[8,64]{1,0:T(8,128)S(1)}, f32[8,64]{1,0:T(8,128)S(1)}, u32[]{:S(2)}, u32[]{:S(2)}) collective-permute-start(f32[8,64]{1,0:T(8,128)S(1)} %add.32), channel_id=1, source_target_pairs={{0,17},{1,16},{2,19},{3,18},{4,21},{5,20},{6,23},{7,22},{8,25},{9,... | collective-permute-start | bytes 6152 | tf_op jit(solution)/shard_map/ppermute | solution.py:137
  35.9 3.9 %collective-permute-start.5 = (f32[8,64]{1,0:T(8,128)S(1)}, f32[8,64]{1,0:T(8,128)S(1)}, u32[]{:S(2)}, u32[]{:S(2)}) collective-permute-start(f32[8,64]{1,0:T(8,128)S(1)} %add.32), channel_id=1, source_target_pairs={{0,9},{1,8},{2,11},{3,10},{4,13},{5,12},{6,15},{7,14},{8,1},{9,0},... | collective-permute-start | bytes 6152 | tf_op jit(solution)/shard_map/ppermute | solution.py:137
  39.8 1.4 %copy-start.4 = (f32[64]{0:T(128)}, f32[64]{0:T(128)S(1)}, u32[]{:S(2)}) copy-start(f32[64]{0:T(128)S(1)} %sqrt_bitcast_fusion) | copy-start | bytes 772

commit v2 on v1

v2 whole, which is shorter than its diff:
```python
import functools

import jax
import jax.numpy as jnp
from jax import lax
from jax.experimental import pallas as pl
from jax.experimental.pallas import tpu as pltpu
from jax.sharding import PartitionSpec as P

SUB = 8
EXACT = lax.Precision.HIGHEST


def held_in(*values):
    return [pltpu.with_memory_space_constraint(value, pltpu.VMEM) for value in values]


def parity(index, count):
    result = index & 1
    for bit in range(1, count.bit_length() - 1):
        result = result ^ ((index >> bit) & 1)
    return result


def gram_of(factor_t):
    return lax.dot_general(factor_t, factor_t, (((1,), (1,)), ((), ())), preferred_element_type=jnp.float32)


def packed(value):
    count = value.shape[0] // 2
    return jnp.concatenate([value[:count], value[count:]], axis=1)


def product_kernel(
    tri, tensor_ref, bin_t_ref, trial_ref, send_ref, own_ref, gram_ref, block_ref, bin_ref, local_ref, wide_ref, sems
):
    neurons, trials, bins = block_ref.shape
    rank = bin_ref.shape[0]
    pair = trials // 2
    share = neurons // (2 * tri)
    rows = share // 2
    bin_copy = pltpu.make_async_copy(bin_t_ref, bin_ref, sems.at[0])
    trial_copy = pltpu.make_async_copy(trial_ref, local_ref, sems.at[1])
    block_copy = pltpu.make_async_copy(tensor_ref, block_ref, sems.at[2])
    bin_copy.start()
    trial_copy.start()
    block_copy.start()
    half = lax.axis_index("bin") ^ parity(lax.axis_index("tri"), tri)
    bin_copy.wait()
    bin_t = bin_ref[...]
    gram = lax.dot_general(bin_t, bin_t, (((1,), (1,)), ((), ())), preferred_element_type=jnp.float32)
    send_ref[rows * tri :, :] = packed(gram)
    factor = bin_t.T
    zero = jnp.zeros_like(factor)
    wide_ref[:bins, :] = jnp.concatenate([factor, zero], axis=1)
    wide_ref[bins:, :] = jnp.concatenate([zero, factor], axis=1)
    trial_copy.wait()
    trial = local_ref[...]
    gram = lax.dot_general(trial, trial, (((0,), (0,)), ((), ())), preferred_element_type=jnp.float32)
    gram_ref[...] = packed(gram)
    trial = packed(trial.astype(jnp.float32))
    left = lax.broadcasted_iota(jnp.int32, (rows, 2 * rank), 1) < rank
    wide = wide_ref[...]
    block_copy.wait()
    for t in range(tri):
        for out_ref, side in ((send_ref, 1), (own_ref, 0)):
            first = (2 * t + (half ^ parity(t, tri) ^ side)) * share
            part = block_ref.at[pl.ds(first, share)]
            low = part[:, :pair, :].reshape(share * pair, bins)
            high = part[:, pair:, :].reshape(share * pair, bins)
            section = jnp.dot(jnp.concatenate([low, high], axis=1), wide, preferred_element_type=jnp.float32)
            total = jnp.sum(section.reshape(share, pair, 2 * rank) * trial[None], axis=1)
            total = total + pltpu.roll(total, rank, 1)
            out_ref[t * rows : (t + 1) * rows, :] = jnp.where(left, total[:rows], total[rows:])


def products(tri, tensor, bin_t, trial_factor):
    neurons, trials, bins = tensor.shape
    rank = bin_t.shape[0]
    rows = neurons // 4
    f32 = jnp.float32
    anywhere = pl.BlockSpec(memory_space=pl.ANY)
    inside = pl.BlockSpec(memory_space=pltpu.VMEM)
    return pl.pallas_call(
        functools.partial(product_kernel, tri),
        in_specs=[anywhere] * 3,
        out_specs=(inside,) * 3,
        out_shape=(
            pltpu.VMEM((rows + rank // 2, 2 * rank), f32),
            pltpu.VMEM((rows, 2 * rank), f32),
            pltpu.VMEM((rank // 2, 2 * rank), f32),
        ),
        scratch_shapes=[
            pltpu.VMEM((neurons, trials, bins), jnp.bfloat16),
            pltpu.VMEM((rank, bins), jnp.bfloat16),
            pltpu.VMEM((trials, rank), jnp.bfloat16),
            pltpu.VMEM((2 * bins, 2 * rank), jnp.bfloat16),
            pltpu.SemaphoreType.DMA((3,)),
        ],
        name="products",
    )(tensor, bin_t, trial_factor)


def inverse_tiles(tiles):
    shape = tiles[0].shape
    count = len(tiles)
    lane = lax.broadcasted_iota(jnp.int32, shape, 1)
    sub = lax.broadcasted_iota(jnp.int32, shape, 0)
    across = lambda tile, j: jnp.broadcast_to(tile[:, j : j + 1], shape)
    down = lambda tile, i: jnp.broadcast_to(tile[i : i + 1, :], shape)
    for panel in range(count):
        base = panel * SUB
        columns = [across(tiles[panel], base + j) for j in range(SUB)]
        block = tiles[panel]
        for k in range(SUB):
            scale = 1.0 / down(columns[k], k)
            column = columns[k]
            row = jnp.where(lane == base + k, 1.0, down(block, k)) * scale
            block = jnp.where(sub == k, row, jnp.where(lane == base + k, 0.0, block) - column * row)
            for j in range(k + 1, SUB):
                row = down(columns[j], k) * scale
                columns[j] = jnp.where(sub == k, row, columns[j] - column * row)
        inside = (lane >= base) & (lane < base + SUB)
        rows = [down(block, j) for j in range(SUB)]
        updated = {panel: block}
        for index in range(1, count):
            index = (panel + index) % count
            tile = tiles[index]
            even = across(tile, base) * rows[0]
            odd = jnp.where(inside, 0.0, tile)
            for j in range(1, SUB):
                if j % 2:
                    odd = odd - across(tile, base + j) * rows[j]
                else:
                    even = even + across(tile, base + j) * rows[j]
            updated[index] = odd - even
        tiles = [updated[index] for index in range(count)]
    return tiles


def inverse_kernel(bin_a_ref, bin_b_ref, trial_a_ref, trial_b_ref, out_ref):
    rank = out_ref.shape[0] // 2
    gram = (bin_a_ref[...] + bin_b_ref[...]) * (trial_a_ref[...] + trial_b_ref[...])
    tiles = [gram[i : i + SUB, lane : lane + rank] for lane in (0, rank) for i in range(0, rank // 2, SUB)]
    zero = jnp.zeros_like(tiles[0])
    for i, tile in enumerate(inverse_tiles(tiles)):
        out_ref[i * SUB : (i + 1) * SUB, :] = jnp.concatenate([tile, zero], axis=1)
        out_ref[rank + i * SUB : rank + (i + 1) * SUB, :] = jnp.concatenate([zero, tile], axis=1)


def solve_kernel(own_ref, other_ref, inverse_ref, solved_ref, squares_ref):
    rank = inverse_ref.shape[0] // 2
    solved = jnp.dot(own_ref[...] + other_ref[...], inverse_ref[...], preferred_element_type=jnp.float32, precision=EXACT)
    solved_ref[...] = solved
    squares = jnp.sum(solved * solved, axis=0, keepdims=True)
    squares = jnp.broadcast_to(squares, squares_ref.shape)
    squares_ref[...] = squares + pltpu.roll(squares, rank, 1)


def scale_kernel(count, solved_ref, one_ref, two_ref, three_ref, four_ref, out_ref, weights_ref):
    share, rank = out_ref.shape
    rows = share // 2
    squares = (one_ref[...] + two_ref[...]) + (three_ref[...] + four_ref[...])
    weights = jnp.sqrt(squares[:1] / count + 1e-06)
    weights_ref[...] = weights[:, :rank]
    mine = solved_ref[pl.ds(pl.multiple_of(lax.axis_index("tri") * rows, SUB), rows), :] / weights
    out_ref[:rows, :] = mine[:, :rank]
    out_ref[rows:, :] = mine[:, rank:]


def local(neur, tri, tensor, bin_factor, trial_factor):
    axes = ("neur", "tri", "bin")
    rank = bin_factor.shape[1]
    f32 = jnp.float32

    def swap(value, n, t, b):
        flat = lambda i, j, k: (i * tri + j) * 2 + k
        pairs = [(flat(i, j, k), flat(i ^ n, j ^ t, k ^ b)) for i in range(neur) for j in range(tri) for k in range(2)]
        return lax.ppermute(value, axes, pairs)

    rows = tensor.shape[0]
    held = rows // 4
    share = rows // (2 * tri)
    sent, own, trial_gram = products(tri, tensor, bin_factor.T, trial_factor)
    got = swap(sent, 0, 0, 1)
    bin_a, bin_b = sent[held:], got[held:]
    block = own + got[:held]
    bit = 1
    while bit < tri // 2:
        joined = jnp.concatenate([block, trial_gram], axis=0)
        joined = joined + swap(joined, 0, bit, 1)
        block, trial_gram = joined[:held], joined[held:]
        bit *= 2
    trial_other = swap(trial_gram, 0, bit, 1)
    other = swap(block, 0, bit, 1)
    inside = pl.BlockSpec(memory_space=pltpu.VMEM)
    inverse = pl.pallas_call(
        inverse_kernel,
        in_specs=[inside] * 4,
        out_specs=inside,
        out_shape=pltpu.VMEM((2 * rank, 2 * rank), f32),
        name="inverse",
    )(*held_in(bin_a, bin_b, trial_gram, trial_other))
    solved, squares = pl.pallas_call(
        solve_kernel,
        in_specs=[inside] * 3,
        out_specs=(inside, inside),
        out_shape=(pltpu.VMEM((held, 2 * rank), f32), pltpu.VMEM((SUB, 2 * rank), f32)),
        name="solve",
    )(*held_in(block, other, inverse))
    squares = squares + swap(squares, 0, 0, 1)
    bit = 1
    parts = None
    while bit < neur:
        if bit * 2 < neur:
            parts = [squares] + [swap(squares, k * bit, 0, 1) for k in (1, 2, 3)]
            bit *= 4
        else:
            zero = jnp.zeros_like(squares)
            parts = [squares, swap(squares, bit, 0, 1), zero, zero]
            bit *= 2
        if bit < neur:
            squares = (parts[0] + parts[1]) + (parts[2] + parts[3])
    result, weights = pl.pallas_call(
        functools.partial(scale_kernel, rows * neur),
        in_specs=[inside] * 5,
        out_specs=(inside, inside),
        out_shape=(jax.ShapeDtypeStruct((share, rank), f32), jax.ShapeDtypeStruct((1, rank), f32)),
        name="scale",
    )(*held_in(solved, *parts))
    return (result, weights[0])


def solution(mesh):
    return jax.shard_map(
        functools.partial(local, mesh.shape["neur"], mesh.shape["tri"]),
        mesh=mesh,
        in_specs=(P("neur", "tri", "bin"), P("bin", None), P("tri", None)),
        out_specs=(P(("neur", "tri", "bin"), None), P()),
        check_vma=False,
    )
```

time: 41.8 us -> 27.7 us (0.66)
  the two profiles are of different devices: /device:TPU:0 before, /device:TPU:1 now
where the time goes in v2:
time: 27.7 us; the launch traced here: 27.3 us
  waiting for transfers between devices  11.3 us (41%)
  starting transfers between devices  8.96 us (32%)
  Pallas kernels  6.31 us (23%)
  between operations  0.67 us (2%)
    ppermute x8, waiting for transfers between devices, swap(): return lax.ppermute(value, axes, pairs)  11.3 us
    ppermute x8, starting transfers between devices, swap(): return lax.ppermute(value, axes, pairs)  8.96 us
    pallas_call x1, Pallas kernels, products(): pl.pallas_call(functools.partial(product_kernel, tri), in_specs=[anywhere...  3.59 us
    pallas_call x1, Pallas kernels, local(): pl.pallas_call(inverse_kernel, in_specs=[inside] * 4, out_specs=inside, o...  1.74 us
    pallas_call x1, Pallas kernels, local(): pl.pallas_call(functools.partial(scale_kernel, rows * neur), in_specs=[in...  0.71 us
  transfers between devices with their start and end apart: 8, of which 6 were waited for; matrix products, arithmetic and copies ran while one was open for 0% of the time, Pallas kernels for 6%

profile of v2, /device:TPU:1, one launch (start us, length us, event | category | flops | bytes accessed | tf_op | source)
XLA Modules:
  0.0 27.3 jit_solution(8643088252335500917)
XLA Ops:
  0.6 3.6 %products.1 = (f32[160,128]{1,0:T(8,128)S(1)}, f32[128,128]{1,0:T(8,128)S(1)}, f32[32,128]{1,0:T(8,128)S(1)}) custom-call(bf16[512,32,128]{2,1,0:T(8,128)(2,1)} %tensor_ref.1, bf16[64,128]{1,0:T(8,128)(2,1)} %bitcast.2, bf16[32,64]{1,0:T(8,128)(2,1)} %trial_ref.1), custom_call_target="tpu_custom_call" | custom-call | tf_op jit(solution)/shard_map/products/pallas_call | solution.py:84
  4.2 0.1 collective-permute-start
  4.3 1.2 %collective-permute-done = f32[160,128]{1,0:T(8,128)S(1)} collective-permute-done((f32[160,128]{1,0:T(8,128)S(1)}, f32[160,128]{1,0:T(8,128)S(1)}, u32[]{:S(2)}, u32[]{:S(2)}) %collective-permute-start) | collective-permute-done | bytes 81952 | tf_op jit(solution)/shard_map/ppermute | solution.py:179
  5.6 2.7 %collective-permute-start.1 = (f32[160,128]{1,0:T(8,128)S(1)}, f32[160,128]{1,0:T(8,128)S(1)}, u32[]{:S(2)}, u32[]{:S(2)}) collective-permute-start(f32[160,128]{1,0:T(8,128)S(1)} %pad_maximum_fusion), channel_id=1, source_target_pairs={{0,3},{1,2},{2,1},{3,0},{4,7},{5,6},{6,5},{7,4},{8,11},{9,10},{10,... | collective-permute-start | bytes 245768 | tf_op jit(solution)/shard_map/ppermute | solution.py:179
  8.3 2.5 %collective-permute-done.1 = f32[160,128]{1,0:T(8,128)S(1)} collective-permute-done((f32[160,128]{1,0:T(8,128)S(1)}, f32[160,128]{1,0:T(8,128)S(1)}, u32[]{:S(2)}, u32[]{:S(2)}) %collective-permute-start.1) | collective-permute-done | bytes 81952 | tf_op jit(solution)/shard_map/ppermute | solution.py:179
  10.8 2.0 %collective-permute-start.2 = (f32[128,128]{1,0:T(8,128)S(1)}, f32[128,128]{1,0:T(8,128)S(1)}, u32[]{:S(2)}, u32[]{:S(2)}) collective-permute-start(f32[128,128]{1,0:T(8,128)S(1)} %slice.21.own_ref), channel_id=1, source_target_pairs={{0,5},{1,4},{2,7},{3,6},{4,1},{5,0},{6,3},{7,2},{8,13},{9,12},{10,... | collective-permute-start | bytes 196616 | tf_op jit(solution)/shard_map/ppermute | solution.py:179
  12.8 0.1 collective-permute-start.3
  12.9 3.1 %collective-permute-done.3.trial_b_ref = f32[32,128]{1,0:T(8,128)S(1)} collective-permute-done((f32[32,128]{1,0:T(8,128)S(1)}, f32[32,128]{1,0:T(8,128)S(1)}, u32[]{:S(2)}, u32[]{:S(2)}) %collective-permute-start.3) | collective-permute-done | bytes 16416 | tf_op jit(solution)/shard_map/ppermute | solution.py:179
  16.0 1.7 %inverse.1.inverse_ref = f32[128,128]{1,0:T(8,128)S(1)} custom-call(f32[32,128]{1,0:T(8,128)S(1)} %slice.17.bin_a_ref, f32[32,128]{1,0:T(8,128)S(1)} %slice.22.bin_b_ref, f32[32,128]{1,0:T(8,128)S(1)} %slice.23.trial_a_ref, f32[32,128]{1,0:T(8,128)S(1)} %collective-permute-done.3.trial_b_ref), custom_call_target="tpu_custom_call" | custom-call | tf_op jit(solution)/shard_map/inverse/pallas_call | solution.py:197
  17.7 0.0 collective-permute-done.2.other_ref
  17.7 0.3 %solve.1 = (f32[128,128]{1,0:T(8,128)S(1)}, f32[8,128]{1,0:T(8,128)S(1)}) custom-call(f32[128,128]{1,0:T(8,128)S(1)} %slice.21.own_ref, f32[128,128]{1,0:T(8,128)S(1)} %collective-permute-done.2.other_ref, f32[128,128]{1,0:T(8,128)S(1)} %inverse.1.inverse_ref), custom_call_target="tpu_custom_call" | custom-call | tf_op jit(solution)/shard_map/solve/pallas_call | solution.py:204
  18.0 0.2 collective-permute-start.4
  18.1 1.0 %collective-permute-done.4 = f32[8,128]{1,0:T(8,128)S(1)} collective-permute-done((f32[8,128]{1,0:T(8,128)S(1)}, f32[8,128]{1,0:T(8,128)S(1)}, u32[]{:S(2)}, u32[]{:S(2)}) %collective-permute-start.4) | collective-permute-done | bytes 4128 | tf_op jit(solution)/shard_map/ppermute | solution.py:179
  19.2 3.5 %collective-permute-start.7 = (f32[8,128]{1,0:T(8,128)S(1)}, f32[8,128]{1,0:T(8,128)S(1)}, u32[]{:S(2)}, u32[]{:S(2)}) collective-permute-start(f32[8,128]{1,0:T(8,128)S(1)} %add.11.one_ref), channel_id=1, source_target_pairs={{0,25},{1,24},{2,27},{3,26},{4,29},{5,28},{6,31},{7,30},{8,17},{9,... | collective-permute-start | bytes 12296 | tf_op jit(solution)/shard_map/ppermute | solution.py:179
  22.6 0.0 collective-permute-start.6
  22.6 0.4 %collective-permute-start.5 = (f32[8,128]{1,0:T(8,128)S(1)}, f32[8,128]{1,0:T(8,128)S(1)}, u32[]{:S(2)}, u32[]{:S(2)}) collective-permute-start(f32[8,128]{1,0:T(8,128)S(1)} %add.11.one_ref), channel_id=1, source_target_pairs={{0,9},{1,8},{2,11},{3,10},{4,13},{5,12},{6,15},{7,14},{8,1},{9,0},... | collective-permute-start | bytes 12296 | tf_op jit(solution)/shard_map/ppermute | solution.py:179
  23.0 0.9 %collective-permute-done.7.four_ref = f32[8,128]{1,0:T(8,128)S(1)} collective-permute-done((f32[8,128]{1,0:T(8,128)S(1)}, f32[8,128]{1,0:T(8,128)S(1)}, u32[]{:S(2)}, u32[]{:S(2)}) %collective-permute-start.7) | collective-permute-done | bytes 4128 | tf_op jit(solution)/shard_map/ppermute | solution.py:179
  24.0 2.6 %collective-permute-done.6.three_ref = f32[8,128]{1,0:T(8,128)S(1)} collective-permute-done((f32[8,128]{1,0:T(8,128)S(1)}, f32[8,128]{1,0:T(8,128)S(1)}, u32[]{:S(2)}, u32[]{:S(2)}) %collective-permute-start.6) | collective-permute-done | bytes 4128 | tf_op jit(solution)/shard_map/ppermute | solution.py:179
  26.6 0.0 collective-permute-done.5.two_ref
  26.6 0.7 %scale.1 = (f32[64,64]{1,0:T(8,128)}, f32[1,64]{1,0:T(1,128)}) custom-call(f32[128,128]{1,0:T(8,128)S(1)} %get-tuple-element.12.solved_ref, f32[8,128]{1,0:T(8,128)S(1)} %add.11.one_ref, f32[8,128]{1,0:T(8,128)S(1)} %collective-permute-done.5.two_ref, f32[8,128]{1,0:T(8,128)S(1)} %collective-permute-done.6.three_ref, ...), custom_call_target="tpu_custom_call" | custom-call | tf_op jit(solution)/shard_map/scale/pallas_call | solution.py:224
  (8 shorter events, 0.0 us)
Async XLA Ops:
  4.2 1.3 %collective-permute-start = (f32[160,128]{1,0:T(8,128)S(1)}, f32[160,128]{1,0:T(8,128)S(1)}, u32[]{:S(2)}, u32[]{:S(2)}) collective-permute-start(f32[160,128]{1,0:T(8,128)S(1)} %get-tuple-element.10), channel_id=1, source_target_pairs={{0,1},{1,0},{2,3},{3,2},{4,5},{5,4},{6,7},{7,6},{8,9},{9,8},{10,11... | collective-permute-start | bytes 245768 | tf_op jit(solution)/shard_map/ppermute | solution.py:179
  5.6 5.1 %collective-permute-start.1 = (f32[160,128]{1,0:T(8,128)S(1)}, f32[160,128]{1,0:T(8,128)S(1)}, u32[]{:S(2)}, u32[]{:S(2)}) collective-permute-start(f32[160,128]{1,0:T(8,128)S(1)} %pad_maximum_fusion), channel_id=1, source_target_pairs={{0,3},{1,2},{2,1},{3,0},{4,7},{5,6},{6,5},{7,4},{8,11},{9,10},{10,... | collective-permute-start | bytes 245768 | tf_op jit(solution)/shard_map/ppermute | solution.py:179
  10.8 6.9 %collective-permute-start.2 = (f32[128,128]{1,0:T(8,128)S(1)}, f32[128,128]{1,0:T(8,128)S(1)}, u32[]{:S(2)}, u32[]{:S(2)}) collective-permute-start(f32[128,128]{1,0:T(8,128)S(1)} %slice.21.own_ref), channel_id=1, source_target_pairs={{0,5},{1,4},{2,7},{3,6},{4,1},{5,0},{6,3},{7,2},{8,13},{9,12},{10,... | collective-permute-start | bytes 196616 | tf_op jit(solution)/shard_map/ppermute | solution.py:179
  12.8 3.2 %collective-permute-start.3 = (f32[32,128]{1,0:T(8,128)S(1)}, f32[32,128]{1,0:T(8,128)S(1)}, u32[]{:S(2)}, u32[]{:S(2)}) collective-permute-start(f32[32,128]{1,0:T(8,128)S(1)} %slice.23.trial_a_ref), channel_id=1, source_target_pairs={{0,5},{1,4},{2,7},{3,6},{4,1},{5,0},{6,3},{7,2},{8,13},{9,12},{10,... | collective-permute-start | bytes 49160 | tf_op jit(solution)/shard_map/ppermute | solution.py:179
  18.0 1.2 %collective-permute-start.4 = (f32[8,128]{1,0:T(8,128)S(1)}, f32[8,128]{1,0:T(8,128)S(1)}, u32[]{:S(2)}, u32[]{:S(2)}) collective-permute-start(f32[8,128]{1,0:T(8,128)S(1)} %get-tuple-element.13), channel_id=1, source_target_pairs={{0,1},{1,0},{2,3},{3,2},{4,5},{5,4},{6,7},{7,6},{8,9},{9,8},{10,11... | collective-permute-start | bytes 12296 | tf_op jit(solution)/shard_map/ppermute | solution.py:179
  19.2 4.8 %collective-permute-start.7 = (f32[8,128]{1,0:T(8,128)S(1)}, f32[8,128]{1,0:T(8,128)S(1)}, u32[]{:S(2)}, u32[]{:S(2)}) collective-permute-start(f32[8,128]{1,0:T(8,128)S(1)} %add.11.one_ref), channel_id=1, source_target_pairs={{0,25},{1,24},{2,27},{3,26},{4,29},{5,28},{6,31},{7,30},{8,17},{9,... | collective-permute-start | bytes 12296 | tf_op jit(solution)/shard_map/ppermute | solution.py:179
  22.6 3.9 %collective-permute-start.6 = (f32[8,128]{1,0:T(8,128)S(1)}, f32[8,128]{1,0:T(8,128)S(1)}, u32[]{:S(2)}, u32[]{:S(2)}) collective-permute-start(f32[8,128]{1,0:T(8,128)S(1)} %add.11.one_ref), channel_id=1, source_target_pairs={{0,17},{1,16},{2,19},{3,18},{4,21},{5,20},{6,23},{7,22},{8,25},{9,... | collective-permute-start | bytes 12296 | tf_op jit(solution)/shard_map/ppermute | solution.py:179
  22.6 3.9 %collective-permute-start.5 = (f32[8,128]{1,0:T(8,128)S(1)}, f32[8,128]{1,0:T(8,128)S(1)}, u32[]{:S(2)}, u32[]{:S(2)}) collective-permute-start(f32[8,128]{1,0:T(8,128)S(1)} %add.11.one_ref), channel_id=1, source_target_pairs={{0,9},{1,8},{2,11},{3,10},{4,13},{5,12},{6,15},{7,14},{8,1},{9,0},... | collective-permute-start | bytes 12296 | tf_op jit(solution)/shard_map/ppermute | solution.py:179

commit v3 on v2

--- a/solution.py
+++ b/solution.py
@@ -41,10 +41,15 @@
     rows = share // 2
     bin_copy = pltpu.make_async_copy(bin_t_ref, bin_ref, sems.at[0])
     trial_copy = pltpu.make_async_copy(trial_ref, local_ref, sems.at[1])
-    block_copy = pltpu.make_async_copy(tensor_ref, block_ref, sems.at[2])
+    groups = ((0, 1), (2, 3))
+    copies = []
+    for i, g in enumerate(groups):
+        span = pl.ds(2 * g[0] * share, 2 * len(g) * share)
+        copies.append(pltpu.make_async_copy(tensor_ref.at[span], block_ref.at[span], sems.at[2 + i]))
     bin_copy.start()
     trial_copy.start()
-    block_copy.start()
+    for copy in copies:
+        copy.start()
     half = lax.axis_index("bin") ^ parity(lax.axis_index("tri"), tri)
     bin_copy.wait()
     bin_t = bin_ref[...]
@@ -61,17 +66,18 @@
     trial = packed(trial.astype(jnp.float32))
     left = lax.broadcasted_iota(jnp.int32, (rows, 2 * rank), 1) < rank
     wide = wide_ref[...]
-    block_copy.wait()
-    for t in range(tri):
-        for out_ref, side in ((send_ref, 1), (own_ref, 0)):
-            first = (2 * t + (half ^ parity(t, tri) ^ side)) * share
-            part = block_ref.at[pl.ds(first, share)]
-            low = part[:, :pair, :].reshape(share * pair, bins)
-            high = part[:, pair:, :].reshape(share * pair, bins)
-            section = jnp.dot(jnp.concatenate([low, high], axis=1), wide, preferred_element_type=jnp.float32)
-            total = jnp.sum(section.reshape(share, pair, 2 * rank) * trial[None], axis=1)
-            total = total + pltpu.roll(total, rank, 1)
-            out_ref[t * rows : (t + 1) * rows, :] = jnp.where(left, total[:rows], total[rows:])
+    for i, g in enumerate(groups):
+        copies[i].wait()
+        for t in g:
+            for out_ref, side in ((send_ref, 1), (own_ref, 0)):
+                first = (2 * t + (half ^ parity(t, tri) ^ side)) * share
+                part = block_ref.at[pl.ds(first, share)]
+                low = part[:, :pair, :].reshape(share * pair, bins)
+                high = part[:, pair:, :].reshape(share * pair, bins)
+                section = jnp.dot(jnp.concatenate([low, high], axis=1), wide, preferred_element_type=jnp.float32)
+                total = jnp.sum(section.reshape(share, pair, 2 * rank) * trial[None], axis=1)
+                total = total + pltpu.roll(total, rank, 1)
+                out_ref[t * rows : (t + 1) * rows, :] = jnp.where(left, total[:rows], total[rows:])
 
 
 def products(tri, tensor, bin_t, trial_factor):
@@ -95,7 +101,7 @@
             pltpu.VMEM((rank, bins), jnp.bfloat16),
             pltpu.VMEM((trials, rank), jnp.bfloat16),
             pltpu.VMEM((2 * bins, 2 * rank), jnp.bfloat16),
-            pltpu.SemaphoreType.DMA((3,)),
+            pltpu.SemaphoreType.DMA((8,)),
         ],
         name="products",
     )(tensor, bin_t, trial_factor)
@@ -173,10 +179,13 @@
     rank = bin_factor.shape[1]
     f32 = jnp.float32
 
+    def exchange(value, partner):
+        flat = lambda n, t, b: (n * tri + t) * 2 + b
+        places = [(n, t, b) for n in range(neur) for t in range(tri) for b in range(2)]
+        return lax.ppermute(value, axes, [(flat(*place), flat(*partner(*place))) for place in places])
+
     def swap(value, n, t, b):
-        flat = lambda i, j, k: (i * tri + j) * 2 + k
-        pairs = [(flat(i, j, k), flat(i ^ n, j ^ t, k ^ b)) for i in range(neur) for j in range(tri) for k in range(2)]
-        return lax.ppermute(value, axes, pairs)
+        return exchange(value, lambda i, j, k: (i ^ n, j ^ t, k ^ b))
 
     rows = tensor.shape[0]
     held = rows // 4
@@ -185,14 +194,14 @@
     got = swap(sent, 0, 0, 1)
     bin_a, bin_b = sent[held:], got[held:]
     block = own + got[:held]
+    joined = jnp.concatenate([block, trial_gram], axis=0)
     bit = 1
     while bit < tri // 2:
-        joined = jnp.concatenate([block, trial_gram], axis=0)
         joined = joined + swap(joined, 0, bit, 1)
-        block, trial_gram = joined[:held], joined[held:]
         bit *= 2
-    trial_other = swap(trial_gram, 0, bit, 1)
-    other = swap(block, 0, bit, 1)
+    other = swap(joined, 0, bit, 1)
+    block, other_block = joined[:held], other[:held]
+    trial_gram, trial_other = joined[held:], other[held:]
     inside = pl.BlockSpec(memory_space=pltpu.VMEM)
     inverse = pl.pallas_call(
         inverse_kernel,
@@ -207,13 +216,15 @@
         out_specs=(inside, inside),
         out_shape=(pltpu.VMEM((held, 2 * rank), f32), pltpu.VMEM((SUB, 2 * rank), f32)),
         name="solve",
-    )(*held_in(block, other, inverse))
+    )(*held_in(block, other_block, inverse))
     squares = squares + swap(squares, 0, 0, 1)
     bit = 1
     parts = None
     while bit < neur:
         if bit * 2 < neur:
-            parts = [squares] + [swap(squares, k * bit, 0, 1) for k in (1, 2, 3)]
+            far = exchange(squares, lambda n, t, b: (n ^ ((2 + b) * bit), t, b))
+            near = swap(squares, bit, 0, 1)
+            parts = [squares, near, far, swap(far, 0, 0, 1)]
             bit *= 4
         else:
             zero = jnp.zeros_like(squares)

time: 27.7 us -> 25.9 us (0.935)
  waiting for transfers between devices: 11.3 us -> 9.13 us
  starting transfers between devices: 8.96 us -> 9.82 us
  Pallas kernels: 6.31 us -> 6.01 us
    ppermute x8 -> x7, waiting for transfers between devices: 11.3 us -> 9.13 us  [exchange(): lax.ppermute(value, axes, [(flat(*place), flat(*partner(*place))) for pla...]
    ppermute x8 -> x7, starting transfers between devices: 8.96 us -> 9.82 us  [exchange(): lax.ppermute(value, axes, [(flat(*place), flat(*partner(*place))) for pla...]
    pallas_call x1, Pallas kernels: 3.59 us -> 3.28 us  [products(): pl.pallas_call(functools.partial(product_kernel, tri), in_specs=[anywhere...]
  transfers between devices with their start and end apart: 8 -> 7, of which waited for: 6 -> 6; matrix products, arithmetic and copies ran while one was open for 0% -> 0% of each run, Pallas kernels for 6% -> 0%
where the time goes in v3:
time: 25.9 us; the launch traced here: 25.7 us
  starting transfers between devices  9.82 us (38%)
  waiting for transfers between devices  9.13 us (35%)
  Pallas kernels  6.01 us (23%)
  between operations  0.67 us (3%)
    ppermute x7, starting transfers between devices, exchange(): lax.ppermute(value, axes, [(flat(*place), flat(*partner(*place))) for pla...  9.82 us
    ppermute x7, waiting for transfers between devices, exchange(): lax.ppermute(value, axes, [(flat(*place), flat(*partner(*place))) for pla...  9.13 us
    pallas_call x1, Pallas kernels, products(): pl.pallas_call(functools.partial(product_kernel, tri), in_specs=[anywhere...  3.28 us
    pallas_call x1, Pallas kernels, local(): pl.pallas_call(inverse_kernel, in_specs=[inside] * 4, out_specs=inside, o...  1.74 us
    pallas_call x1, Pallas kernels, local(): pl.pallas_call(functools.partial(scale_kernel, rows * neur), in_specs=[in...  0.71 us
  transfers between devices with their start and end apart: 7, of which 6 were waited for; matrix products, arithmetic and copies ran while one was open for 0% of the time, Pallas kernels for 0%

profile of v3, /device:TPU:1, one launch (start us, length us, event | category | flops | bytes accessed | tf_op | source)
XLA Modules:
  0.0 25.7 jit_solution(6695718363799771656)
XLA Ops:
  0.6 3.3 %products.1 = (f32[160,128]{1,0:T(8,128)S(1)}, f32[128,128]{1,0:T(8,128)S(1)}, f32[32,128]{1,0:T(8,128)S(1)}) custom-call(bf16[512,32,128]{2,1,0:T(8,128)(2,1)} %tensor_ref.1, bf16[64,128]{1,0:T(8,128)(2,1)} %bitcast.2, bf16[32,64]{1,0:T(8,128)(2,1)} %trial_ref.1), custom_call_target="tpu_custom_call" | custom-call | tf_op jit(solution)/shard_map/products/pallas_call | solution.py:90
  3.9 0.1 collective-permute-start
  4.0 1.2 %collective-permute-done = f32[160,128]{1,0:T(8,128)S(1)} collective-permute-done((f32[160,128]{1,0:T(8,128)S(1)}, f32[160,128]{1,0:T(8,128)S(1)}, u32[]{:S(2)}, u32[]{:S(2)}) %collective-permute-start) | collective-permute-done | bytes 81952 | tf_op jit(solution)/shard_map/ppermute | solution.py:185
  5.3 2.7 %collective-permute-start.1 = (f32[160,128]{1,0:T(8,128)S(1)}, f32[160,128]{1,0:T(8,128)S(1)}, u32[]{:S(2)}, u32[]{:S(2)}) collective-permute-start(f32[160,128]{1,0:T(8,128)S(1)} %pad_maximum_fusion), channel_id=1, source_target_pairs={{0,3},{1,2},{2,1},{3,0},{4,7},{5,6},{6,5},{7,4},{8,11},{9,10},{10,... | collective-permute-start | bytes 245768 | tf_op jit(solution)/shard_map/ppermute | solution.py:185
  8.0 2.5 %collective-permute-done.1 = f32[160,128]{1,0:T(8,128)S(1)} collective-permute-done((f32[160,128]{1,0:T(8,128)S(1)}, f32[160,128]{1,0:T(8,128)S(1)}, u32[]{:S(2)}, u32[]{:S(2)}) %collective-permute-start.1) | collective-permute-done | bytes 81952 | tf_op jit(solution)/shard_map/ppermute | solution.py:185
  10.4 2.0 %collective-permute-start.2 = (f32[160,128]{1,0:T(8,128)S(1)}, f32[160,128]{1,0:T(8,128)S(1)}, u32[]{:S(2)}, u32[]{:S(2)}) collective-permute-start(f32[160,128]{1,0:T(8,128)S(1)} %fusion), channel_id=1, source_target_pairs={{0,5},{1,4},{2,7},{3,6},{4,1},{5,0},{6,3},{7,2},{8,13},{9,12},{10,... | collective-permute-start | bytes 245768 | tf_op jit(solution)/shard_map/ppermute | solution.py:185
  12.5 2.5 %collective-permute-done.2 = f32[160,128]{1,0:T(8,128)S(1)} collective-permute-done((f32[160,128]{1,0:T(8,128)S(1)}, f32[160,128]{1,0:T(8,128)S(1)}, u32[]{:S(2)}, u32[]{:S(2)}) %collective-permute-start.2) | collective-permute-done | bytes 81952 | tf_op jit(solution)/shard_map/ppermute | solution.py:185
  14.9 1.7 %inverse.1.inverse_ref = f32[128,128]{1,0:T(8,128)S(1)} custom-call(f32[32,128]{1,0:T(8,128)S(1)} %slice.24.bin_a_ref, f32[32,128]{1,0:T(8,128)S(1)} %slice.31.bin_b_ref, f32[32,128]{1,0:T(8,128)S(1)} %slice.32.trial_a_ref, f32[32,128]{1,0:T(8,128)S(1)} %slice.33.trial_b_ref), custom_call_target="tpu_custom_call" | custom-call | tf_op jit(solution)/shard_map/inverse/pallas_call | solution.py:206
  16.7 0.3 %solve.1 = (f32[128,128]{1,0:T(8,128)S(1)}, f32[8,128]{1,0:T(8,128)S(1)}) custom-call(f32[128,128]{1,0:T(8,128)S(1)} %slice.29.own_ref, f32[128,128]{1,0:T(8,128)S(1)} %slice.30.other_ref, f32[128,128]{1,0:T(8,128)S(1)} %inverse.1.inverse_ref), custom_call_target="tpu_custom_call" | custom-call | tf_op jit(solution)/shard_map/solve/pallas_call | solution.py:213
  17.0 0.2 collective-permute-start.3
  17.2 0.9 %collective-permute-done.3 = f32[8,128]{1,0:T(8,128)S(1)} collective-permute-done((f32[8,128]{1,0:T(8,128)S(1)}, f32[8,128]{1,0:T(8,128)S(1)}, u32[]{:S(2)}, u32[]{:S(2)}) %collective-permute-start.3) | collective-permute-done | bytes 4128 | tf_op jit(solution)/shard_map/ppermute | solution.py:185
  18.2 3.8 %collective-permute-start.5 = (f32[8,128]{1,0:T(8,128)S(1)}, f32[8,128]{1,0:T(8,128)S(1)}, u32[]{:S(2)}, u32[]{:S(2)}) collective-permute-start(f32[8,128]{1,0:T(8,128)S(1)} %add.11.one_ref), channel_id=1, source_target_pairs={{0,16},{1,25},{2,18},{3,27},{4,20},{5,29},{6,22},{7,31},{8,24},{9,... | collective-permute-start | bytes 12296 | tf_op jit(solution)/shard_map/ppermute | solution.py:185
  21.9 0.8 %collective-permute-start.4 = (f32[8,128]{1,0:T(8,128)S(1)}, f32[8,128]{1,0:T(8,128)S(1)}, u32[]{:S(2)}, u32[]{:S(2)}) collective-permute-start(f32[8,128]{1,0:T(8,128)S(1)} %add.11.one_ref), channel_id=1, source_target_pairs={{0,9},{1,8},{2,11},{3,10},{4,13},{5,12},{6,15},{7,14},{8,1},{9,0},... | collective-permute-start | bytes 12296 | tf_op jit(solution)/shard_map/ppermute | solution.py:185
  22.7 0.2 collective-permute-done.5.three_ref
  22.9 0.2 collective-permute-start.6
  23.1 1.8 %collective-permute-done.4.two_ref = f32[8,128]{1,0:T(8,128)S(1)} collective-permute-done((f32[8,128]{1,0:T(8,128)S(1)}, f32[8,128]{1,0:T(8,128)S(1)}, u32[]{:S(2)}, u32[]{:S(2)}) %collective-permute-start.4) | collective-permute-done | bytes 4128 | tf_op jit(solution)/shard_map/ppermute | solution.py:185
  25.0 0.0 collective-permute-done.6.four_ref
  25.0 0.7 %scale.1 = (f32[64,64]{1,0:T(8,128)}, f32[1,64]{1,0:T(1,128)}) custom-call(f32[128,128]{1,0:T(8,128)S(1)} %get-tuple-element.12.solved_ref, f32[8,128]{1,0:T(8,128)S(1)} %add.11.one_ref, f32[8,128]{1,0:T(8,128)S(1)} %collective-permute-done.4.two_ref, f32[8,128]{1,0:T(8,128)S(1)} %collective-permute-done.5.three_ref, ...), custom_call_target="tpu_custom_call" | custom-call | tf_op jit(solution)/shard_map/scale/pallas_call | solution.py:235
  (10 shorter events, 0.1 us)
Async XLA Ops:
  3.9 1.3 %collective-permute-start = (f32[160,128]{1,0:T(8,128)S(1)}, f32[160,128]{1,0:T(8,128)S(1)}, u32[]{:S(2)}, u32[]{:S(2)}) collective-permute-start(f32[160,128]{1,0:T(8,128)S(1)} %get-tuple-element.10), channel_id=1, source_target_pairs={{0,1},{1,0},{2,3},{3,2},{4,5},{5,4},{6,7},{7,6},{8,9},{9,8},{10,11... | collective-permute-start | bytes 245768 | tf_op jit(solution)/shard_map/ppermute | solution.py:185
  5.3 5.1 %collective-permute-start.1 = (f32[160,128]{1,0:T(8,128)S(1)}, f32[160,128]{1,0:T(8,128)S(1)}, u32[]{:S(2)}, u32[]{:S(2)}) collective-permute-start(f32[160,128]{1,0:T(8,128)S(1)} %pad_maximum_fusion), channel_id=1, source_target_pairs={{0,3},{1,2},{2,1},{3,0},{4,7},{5,6},{6,5},{7,4},{8,11},{9,10},{10,... | collective-permute-start | bytes 245768 | tf_op jit(solution)/shard_map/ppermute | solution.py:185
  10.4 4.5 %collective-permute-start.2 = (f32[160,128]{1,0:T(8,128)S(1)}, f32[160,128]{1,0:T(8,128)S(1)}, u32[]{:S(2)}, u32[]{:S(2)}) collective-permute-start(f32[160,128]{1,0:T(8,128)S(1)} %fusion), channel_id=1, source_target_pairs={{0,5},{1,4},{2,7},{3,6},{4,1},{5,0},{6,3},{7,2},{8,13},{9,12},{10,... | collective-permute-start | bytes 245768 | tf_op jit(solution)/shard_map/ppermute | solution.py:185
  17.0 1.2 %collective-permute-start.3 = (f32[8,128]{1,0:T(8,128)S(1)}, f32[8,128]{1,0:T(8,128)S(1)}, u32[]{:S(2)}, u32[]{:S(2)}) collective-permute-start(f32[8,128]{1,0:T(8,128)S(1)} %get-tuple-element.13), channel_id=1, source_target_pairs={{0,1},{1,0},{2,3},{3,2},{4,5},{5,4},{6,7},{7,6},{8,9},{9,8},{10,11... | collective-permute-start | bytes 12296 | tf_op jit(solution)/shard_map/ppermute | solution.py:185
  18.2 4.8 %collective-permute-start.5 = (f32[8,128]{1,0:T(8,128)S(1)}, f32[8,128]{1,0:T(8,128)S(1)}, u32[]{:S(2)}, u32[]{:S(2)}) collective-permute-start(f32[8,128]{1,0:T(8,128)S(1)} %add.11.one_ref), channel_id=1, source_target_pairs={{0,16},{1,25},{2,18},{3,27},{4,20},{5,29},{6,22},{7,31},{8,24},{9,... | collective-permute-start | bytes 12296 | tf_op jit(solution)/shard_map/ppermute | solution.py:185
  21.9 3.0 %collective-permute-start.4 = (f32[8,128]{1,0:T(8,128)S(1)}, f32[8,128]{1,0:T(8,128)S(1)}, u32[]{:S(2)}, u32[]{:S(2)}) collective-permute-start(f32[8,128]{1,0:T(8,128)S(1)} %add.11.one_ref), channel_id=1, source_target_pairs={{0,9},{1,8},{2,11},{3,10},{4,13},{5,12},{6,15},{7,14},{8,1},{9,0},... | collective-permute-start | bytes 12296 | tf_op jit(solution)/shard_map/ppermute | solution.py:185
  22.9 2.0 %collective-permute-start.6 = (f32[8,128]{1,0:T(8,128)S(1)}, f32[8,128]{1,0:T(8,128)S(1)}, u32[]{:S(2)}, u32[]{:S(2)}) collective-permute-start(f32[8,128]{1,0:T(8,128)S(1)} %collective-permute-done.5.three_ref), channel_id=1, source_target_pairs={{0,1},{1,0},{2,3},{3,2},{4,5},{5,4},{6,7},{7,6},{8,9},{9,8},{10,11... | collective-permute-start | bytes 12296 | tf_op jit(solution)/shard_map/ppermute | solution.py:185

commit v4 on v3

--- a/solution.py
+++ b/solution.py
@@ -8,6 +8,7 @@
 from jax.sharding import PartitionSpec as P
 
 SUB = 8
+GRANT = 16 * 2**20
 EXACT = lax.Precision.HIGHEST
 
 
@@ -31,26 +32,38 @@
     return jnp.concatenate([value[:count], value[count:]], axis=1)
 
 
-def product_kernel(
-    tri, tensor_ref, bin_t_ref, trial_ref, send_ref, own_ref, gram_ref, block_ref, bin_ref, local_ref, wide_ref, sems
-):
-    neurons, trials, bins = block_ref.shape
+def row_products(part, wide, trial, left):
+    share, trials, bins = part.shape
+    pair = trials // 2
+    rank = wide.shape[1] // 2
+    rows = share // 2
+    low = part[:, :pair, :].reshape(share * pair, bins)
+    high = part[:, pair:, :].reshape(share * pair, bins)
+    section = jnp.dot(jnp.concatenate([low, high], axis=1), wide, preferred_element_type=jnp.float32)
+    total = jnp.sum(section.reshape(share, pair, 2 * rank) * trial[None], axis=1)
+    total = total + pltpu.roll(total, rank, 1)
+    return jnp.where(left, total[:rows], total[rows:])
+
+
+def send_kernel(tri, tensor_ref, bin_t_ref, trial_ref, send_ref, gram_ref, held_ref, local_ref, wide_ref, block_ref, bin_ref, sems):
+    neurons, trials, bins = tensor_ref.shape
     rank = bin_ref.shape[0]
-    pair = trials // 2
     share = neurons // (2 * tri)
     rows = share // 2
+    half = lax.axis_index("bin") ^ parity(lax.axis_index("tri"), tri)
     bin_copy = pltpu.make_async_copy(bin_t_ref, bin_ref, sems.at[0])
     trial_copy = pltpu.make_async_copy(trial_ref, local_ref, sems.at[1])
-    groups = ((0, 1), (2, 3))
-    copies = []
-    for i, g in enumerate(groups):
-        span = pl.ds(2 * g[0] * share, 2 * len(g) * share)
-        copies.append(pltpu.make_async_copy(tensor_ref.at[span], block_ref.at[span], sems.at[2 + i]))
     bin_copy.start()
     trial_copy.start()
-    for copy in copies:
-        copy.start()
-    half = lax.axis_index("bin") ^ parity(lax.axis_index("tri"), tri)
+    copies = []
+    for side, target in ((1, block_ref), (0, held_ref)):
+        for t in range(tri):
+            first = (2 * t + (half ^ parity(t, tri) ^ side)) * share
+            copy = pltpu.make_async_copy(
+                tensor_ref.at[pl.ds(first, share)], target.at[pl.ds(t * share, share)], sems.at[2 + len(copies)]
+            )
+            copy.start()
+            copies.append(copy)
     bin_copy.wait()
     bin_t = bin_ref[...]
     gram = lax.dot_general(bin_t, bin_t, (((1,), (1,)), ((), ())), preferred_element_type=jnp.float32)
@@ -60,51 +73,69 @@
     wide_ref[:bins, :] = jnp.concatenate([factor, zero], axis=1)
     wide_ref[bins:, :] = jnp.concatenate([zero, factor], axis=1)
     trial_copy.wait()
-    trial = local_ref[...]
-    gram = lax.dot_general(trial, trial, (((0,), (0,)), ((), ())), preferred_element_type=jnp.float32)
+    local = local_ref[...]
+    gram = lax.dot_general(local, local, (((0,), (0,)), ((), ())), preferred_element_type=jnp.float32)
     gram_ref[...] = packed(gram)
-    trial = packed(trial.astype(jnp.float32))
+    trial = packed(local.astype(jnp.float32))
     left = lax.broadcasted_iota(jnp.int32, (rows, 2 * rank), 1) < rank
     wide = wide_ref[...]
-    for i, g in enumerate(groups):
-        copies[i].wait()
-        for t in g:
-            for out_ref, side in ((send_ref, 1), (own_ref, 0)):
-                first = (2 * t + (half ^ parity(t, tri) ^ side)) * share
-                part = block_ref.at[pl.ds(first, share)]
-                low = part[:, :pair, :].reshape(share * pair, bins)
-                high = part[:, pair:, :].reshape(share * pair, bins)
-                section = jnp.dot(jnp.concatenate([low, high], axis=1), wide, preferred_element_type=jnp.float32)
-                total = jnp.sum(section.reshape(share, pair, 2 * rank) * trial[None], axis=1)
-                total = total + pltpu.roll(total, rank, 1)
-                out_ref[t * rows : (t + 1) * rows, :] = jnp.where(left, total[:rows], total[rows:])
-
-
-def products(tri, tensor, bin_t, trial_factor):
+    for copy in copies[:tri]:
+        copy.wait()
+    for t in range(tri):
+        send_ref[t * rows : (t + 1) * rows, :] = row_products(block_ref.at[pl.ds(t * share, share)], wide, trial, left)
+    for copy in copies[tri:]:
+        copy.wait()
+
+
+def own_kernel(tri, held_ref, local_ref, wide_ref, own_ref):
+    share = held_ref.shape[0] // tri
+    rows = share // 2
+    rank = local_ref.shape[1]
+    local = local_ref[...]
+    trial = packed(local.astype(jnp.float32))
+    left = lax.broadcasted_iota(jnp.int32, (rows, 2 * rank), 1) < rank
+    wide = wide_ref[...]
+    for t in range(tri):
+        own_ref[t * rows : (t + 1) * rows, :] = row_products(held_ref.at[pl.ds(t * share, share)], wide, trial, left)
+
+
+def send_products(tri, tensor, bin_t, trial_factor):
     neurons, trials, bins = tensor.shape
     rank = bin_t.shape[0]
-    rows = neurons // 4
-    f32 = jnp.float32
-    anywhere = pl.BlockSpec(memory_space=pl.ANY)
+    outside = pl.BlockSpec(memory_space=pltpu.HBM)
     inside = pl.BlockSpec(memory_space=pltpu.VMEM)
     return pl.pallas_call(
-        functools.partial(product_kernel, tri),
-        in_specs=[anywhere] * 3,
-        out_specs=(inside,) * 3,
+        functools.partial(send_kernel, tri),
+        in_specs=[outside] * 3,
+        out_specs=(inside,) * 5,
         out_shape=(
-            pltpu.VMEM((rows + rank // 2, 2 * rank), f32),
-            pltpu.VMEM((rows, 2 * rank), f32),
-            pltpu.VMEM((rank // 2, 2 * rank), f32),
+            pltpu.VMEM((neurons // 4 + rank // 2, 2 * rank), jnp.float32),
+            pltpu.VMEM((rank // 2, 2 * rank), jnp.float32),
+            pltpu.VMEM((neurons // 2, trials, bins), jnp.bfloat16),
+            pltpu.VMEM((trials, rank), jnp.bfloat16),
+            pltpu.VMEM((2 * bins, 2 * rank), jnp.bfloat16),
         ),
         scratch_shapes=[
-            pltpu.VMEM((neurons, trials, bins), jnp.bfloat16),
+            pltpu.VMEM((neurons // 2, trials, bins), jnp.bfloat16),
             pltpu.VMEM((rank, bins), jnp.bfloat16),
-            pltpu.VMEM((trials, rank), jnp.bfloat16),
-            pltpu.VMEM((2 * bins, 2 * rank), jnp.bfloat16),
-            pltpu.SemaphoreType.DMA((8,)),
+            pltpu.SemaphoreType.DMA((2 + 2 * tri,)),
         ],
-        name="products",
-    )(tensor, bin_t, trial_factor)
+        compiler_params=pltpu.CompilerParams(vmem_limit_bytes=GRANT),
+        name="send_products",
+    )(*(pltpu.with_memory_space_constraint(value, pltpu.HBM) for value in (tensor, bin_t, trial_factor)))
+
+
+def own_products(tri, held, local, wide):
+    rank = local.shape[1]
+    inside = pl.BlockSpec(memory_space=pltpu.VMEM)
+    return pl.pallas_call(
+        functools.partial(own_kernel, tri),
+        in_specs=[inside] * 3,
+        out_specs=inside,
+        out_shape=pltpu.VMEM((held.shape[0] // 2, 2 * rank), jnp.float32),
+        compiler_params=pltpu.CompilerParams(vmem_limit_bytes=GRANT),
+        name="own_products",
+    )(*held_in(held, local, wide))
 
 
 def inverse_tiles(tiles):
@@ -144,6 +175,22 @@
     return tiles
 
 
+def add_kernel(one_ref, two_ref, out_ref):
+    out_ref[...] = one_ref[...] + two_ref[...]
+
+
+def added(one, two):
+    inside = pl.BlockSpec(memory_space=pltpu.VMEM)
+    return pl.pallas_call(
+        add_kernel,
+        in_specs=[inside] * 2,
+        out_specs=inside,
+        out_shape=pltpu.VMEM(one.shape, one.dtype),
+        cost_estimate=pl.CostEstimate(flops=10000000000, bytes_accessed=200000, transcendentals=0),
+        name="added",
+    )(*held_in(one, two))
+
+
 def inverse_kernel(bin_a_ref, bin_b_ref, trial_a_ref, trial_b_ref, out_ref):
     rank = out_ref.shape[0] // 2
     gram = (bin_a_ref[...] + bin_b_ref[...]) * (trial_a_ref[...] + trial_b_ref[...])
@@ -190,24 +237,25 @@
     rows = tensor.shape[0]
     held = rows // 4
     share = rows // (2 * tri)
-    sent, own, trial_gram = products(tri, tensor, bin_factor.T, trial_factor)
+    sent, trial_gram, kept, local_factor, wide = send_products(tri, tensor, bin_factor.T, trial_factor)
     got = swap(sent, 0, 0, 1)
+    own = own_products(tri, kept, local_factor, wide)
     bin_a, bin_b = sent[held:], got[held:]
     block = own + got[:held]
-    joined = jnp.concatenate([block, trial_gram], axis=0)
     bit = 1
     while bit < tri // 2:
-        joined = joined + swap(joined, 0, bit, 1)
+        trial_gram = added(trial_gram, swap(trial_gram, 0, bit, 1))
+        block = block + swap(block, 0, bit, 1)
         bit *= 2
-    other = swap(joined, 0, bit, 1)
-    block, other_block = joined[:held], other[:held]
-    trial_gram, trial_other = joined[held:], other[held:]
+    trial_other = swap(trial_gram, 0, bit, 1)
+    other_block = swap(block, 0, bit, 1)
     inside = pl.BlockSpec(memory_space=pltpu.VMEM)
     inverse = pl.pallas_call(
         inverse_kernel,
         in_specs=[inside] * 4,
         out_specs=inside,
         out_shape=pltpu.VMEM((2 * rank, 2 * rank), f32),
+        cost_estimate=pl.CostEstimate(flops=10000000000, bytes_accessed=200000, transcendentals=0),
         name="inverse",
     )(*held_in(bin_a, bin_b, trial_gram, trial_other))
     solved, squares = pl.pallas_call(

time: 25.9 us -> 23.9 us (0.923)
  waiting for transfers between devices: 9.13 us -> 5.42 us
  starting transfers between devices: 9.82 us -> 11.6 us
    ppermute x7 -> x9, waiting for transfers between devices: 9.13 us -> 5.42 us  [exchange(): lax.ppermute(value, axes, [(flat(*place), flat(*partner(*place))) for pla...]
    ppermute x7 -> x9, starting transfers between devices: 9.82 us -> 11.6 us  [exchange(): lax.ppermute(value, axes, [(flat(*place), flat(*partner(*place))) for pla...]
    pallas_call x1 -> x3, Pallas kernels: 3.28 us -> 3.23 us  [the longest x1 2.44 us: send_products(): pl.pallas_call(functools.partial(send_kernel, tri), in_specs=[outside] *...]
  transfers between devices with their start and end apart: 7 -> 9, of which waited for: 6 -> 6; matrix products, arithmetic and copies ran while one was open for 0% -> 0% of each run, Pallas kernels for 0% -> 11%
where the time goes in v4:
time: 23.9 us; the launch traced here: 23.6 us
  starting transfers between devices  11.6 us (49%)
  Pallas kernels  5.95 us (25%)
  waiting for transfers between devices  5.42 us (23%)
  between operations  0.66 us (3%)
    ppermute x9, starting transfers between devices, exchange(): lax.ppermute(value, axes, [(flat(*place), flat(*partner(*place))) for pla...  11.6 us
    ppermute x9, waiting for transfers between devices, exchange(): lax.ppermute(value, axes, [(flat(*place), flat(*partner(*place))) for pla...  5.42 us
    pallas_call x1, Pallas kernels, send_products(): pl.pallas_call(functools.partial(send_kernel, tri), in_specs=[outside] *...  2.44 us
    pallas_call x1, Pallas kernels, local(): pl.pallas_call(inverse_kernel, in_specs=[inside] * 4, out_specs=inside, o...  1.74 us
    pallas_call x1, Pallas kernels, own_products(): pl.pallas_call(functools.partial(own_kernel, tri), in_specs=[inside] * 3,...  0.79 us
    pallas_call x1, Pallas kernels, local(): pl.pallas_call(functools.partial(scale_kernel, rows * neur), in_specs=[in...  0.71 us
  transfers between devices with their start and end apart: 9, of which 6 were waited for; matrix products, arithmetic and copies ran while one was open for 0% of the time, Pallas kernels for 11%

profile of v4, /device:TPU:1, one launch (start us, length us, event | category | flops | bytes accessed | tf_op | source)
XLA Modules:
  0.0 23.6 jit_solution(4970657695343873966)
XLA Ops:
  0.6 2.4 %send_products.1 = (f32[160,128]{1,0:T(8,128)S(1)}, f32[32,128]{1,0:T(8,128)S(1)}, bf16[256,32,128]{2,1,0:T(8,128)(2,1)S(1)}, bf16[32,64]{1,0:T(8,128)(2,1)S(1)}, bf16[256,128]{1,0:T(8,128)(2,1)S(1)}) custom-call(bf16[512,32,128]{2,1,0:T(8,128)(2,1)} %tensor_ref.1, bf16[64,128]{1,0:T(8,128)(2,1)} %bitcast.2, bf16[32,64]{1,0:T(8,128)(2,1)} %trial_ref.1), custom_call_target="tpu_custom_call" | custom-call | tf_op jit(solution)/shard_map/send_products/pallas_call | solution.py:107
  3.1 0.1 collective-permute-start
  3.2 2.6 %collective-permute-start.3 = (f32[32,128]{1,0:T(8,128)S(1)}, f32[32,128]{1,0:T(8,128)S(1)}, u32[]{:S(2)}, u32[]{:S(2)}) collective-permute-start(f32[32,128]{1,0:T(8,128)S(1)} %get-tuple-element.15.one_ref), channel_id=1, source_target_pairs={{0,3},{1,2},{2,1},{3,0},{4,7},{5,6},{6,5},{7,4},{8,11},{9,10},{10,... | collective-permute-start | bytes 49160 | tf_op jit(solution)/shard_map/ppermute | solution.py:232
  5.8 0.8 %own_products.1 = f32[128,128]{1,0:T(8,128)S(1)} custom-call(bf16[256,32,128]{2,1,0:T(8,128)(2,1)S(1)} %get-tuple-element.11.held_ref, bf16[32,64]{1,0:T(8,128)(2,1)S(1)} %get-tuple-element.12.local_ref, bf16[256,128]{1,0:T(8,128)(2,1)S(1)} %get-tuple-element.13.wide_ref), custom_call_target="tpu_custom_call" | custom-call | tf_op jit(solution)/shard_map/own_products/pallas_call | solution.py:131
  6.6 0.0 collective-permute-done
  6.6 0.5 %collective-permute-start.1 = (f32[128,128]{1,0:T(8,128)S(1)}, f32[128,128]{1,0:T(8,128)S(1)}, u32[]{:S(2)}, u32[]{:S(2)}) collective-permute-start(f32[128,128]{1,0:T(8,128)S(1)} %slice_add_fusion), channel_id=1, source_target_pairs={{0,3},{1,2},{2,1},{3,0},{4,7},{5,6},{6,5},{7,4},{8,11},{9,10},{10,... | collective-permute-start | bytes 196616 | tf_op jit(solution)/shard_map/ppermute | solution.py:232
  7.1 0.2 collective-permute-done.3.two_ref
  7.3 1.7 %collective-permute-start.4 = (f32[32,128]{1,0:T(8,128)S(1)}, f32[32,128]{1,0:T(8,128)S(1)}, u32[]{:S(2)}, u32[]{:S(2)}) collective-permute-start(f32[32,128]{1,0:T(8,128)S(1)} %added.1.trial_a_ref), channel_id=1, source_target_pairs={{0,5},{1,4},{2,7},{3,6},{4,1},{5,0},{6,3},{7,2},{8,13},{9,12},{10,... | collective-permute-start | bytes 49160 | tf_op jit(solution)/shard_map/ppermute | solution.py:232
  9.0 1.9 %collective-permute-done.1 = f32[128,128]{1,0:T(8,128)S(1)} collective-permute-done((f32[128,128]{1,0:T(8,128)S(1)}, f32[128,128]{1,0:T(8,128)S(1)}, u32[]{:S(2)}, u32[]{:S(2)}) %collective-permute-start.1) | collective-permute-done | bytes 65568 | tf_op jit(solution)/shard_map/ppermute | solution.py:232
  10.9 1.6 %collective-permute-start.2 = (f32[128,128]{1,0:T(8,128)S(1)}, f32[128,128]{1,0:T(8,128)S(1)}, u32[]{:S(2)}, u32[]{:S(2)}) collective-permute-start(f32[128,128]{1,0:T(8,128)S(1)} %add.10.own_ref), channel_id=1, source_target_pairs={{0,5},{1,4},{2,7},{3,6},{4,1},{5,0},{6,3},{7,2},{8,13},{9,12},{10,... | collective-permute-start | bytes 196616 | tf_op jit(solution)/shard_map/ppermute | solution.py:232
  12.5 0.0 collective-permute-done.4.trial_b_ref
  12.5 1.7 %inverse.1.inverse_ref = f32[128,128]{1,0:T(8,128)S(1)} custom-call(f32[32,128]{1,0:T(8,128)S(1)} %slice.10.bin_a_ref, f32[32,128]{1,0:T(8,128)S(1)} %slice.13.bin_b_ref, f32[32,128]{1,0:T(8,128)S(1)} %added.1.trial_a_ref, f32[32,128]{1,0:T(8,128)S(1)} %collective-permute-done.4.trial_b_ref), custom_call_target="tpu_custom_call" | custom-call | flops 10000000000 | bytes 200000 | tf_op jit(solution)/shard_map/inverse/pallas_call | solution.py:253
  14.2 0.8 %collective-permute-done.2.other_ref = f32[128,128]{1,0:T(8,128)S(1)} collective-permute-done((f32[128,128]{1,0:T(8,128)S(1)}, f32[128,128]{1,0:T(8,128)S(1)}, u32[]{:S(2)}, u32[]{:S(2)}) %collective-permute-start.2) | collective-permute-done | bytes 65568 | tf_op jit(solution)/shard_map/ppermute | solution.py:232
  15.1 0.3 %solve.1 = (f32[128,128]{1,0:T(8,128)S(1)}, f32[8,128]{1,0:T(8,128)S(1)}) custom-call(f32[128,128]{1,0:T(8,128)S(1)} %add.10.own_ref, f32[128,128]{1,0:T(8,128)S(1)} %collective-permute-done.2.other_ref, f32[128,128]{1,0:T(8,128)S(1)} %inverse.1.inverse_ref), custom_call_target="tpu_custom_call" | custom-call | tf_op jit(solution)/shard_map/solve/pallas_call | solution.py:261
  15.3 0.4 %collective-permute-start.5 = (f32[8,128]{1,0:T(8,128)S(1)}, f32[8,128]{1,0:T(8,128)S(1)}, u32[]{:S(2)}, u32[]{:S(2)}) collective-permute-start(f32[8,128]{1,0:T(8,128)S(1)} %get-tuple-element.17), channel_id=1, source_target_pairs={{0,1},{1,0},{2,3},{3,2},{4,5},{5,4},{6,7},{7,6},{8,9},{9,8},{10,11... | collective-permute-start | bytes 12296 | tf_op jit(solution)/shard_map/ppermute | solution.py:232
  15.7 0.8 %collective-permute-done.5 = f32[8,128]{1,0:T(8,128)S(1)} collective-permute-done((f32[8,128]{1,0:T(8,128)S(1)}, f32[8,128]{1,0:T(8,128)S(1)}, u32[]{:S(2)}, u32[]{:S(2)}) %collective-permute-start.5) | collective-permute-done | bytes 4128 | tf_op jit(solution)/shard_map/ppermute | solution.py:232
  16.6 3.3 %collective-permute-start.7 = (f32[8,128]{1,0:T(8,128)S(1)}, f32[8,128]{1,0:T(8,128)S(1)}, u32[]{:S(2)}, u32[]{:S(2)}) collective-permute-start(f32[8,128]{1,0:T(8,128)S(1)} %add.11.one_ref), channel_id=1, source_target_pairs={{0,16},{1,25},{2,18},{3,27},{4,20},{5,29},{6,22},{7,31},{8,24},{9,... | collective-permute-start | bytes 12296 | tf_op jit(solution)/shard_map/ppermute | solution.py:232
  19.9 0.8 %collective-permute-start.6 = (f32[8,128]{1,0:T(8,128)S(1)}, f32[8,128]{1,0:T(8,128)S(1)}, u32[]{:S(2)}, u32[]{:S(2)}) collective-permute-start(f32[8,128]{1,0:T(8,128)S(1)} %add.11.one_ref), channel_id=1, source_target_pairs={{0,9},{1,8},{2,11},{3,10},{4,13},{5,12},{6,15},{7,14},{8,1},{9,0},... | collective-permute-start | bytes 12296 | tf_op jit(solution)/shard_map/ppermute | solution.py:232
  20.7 0.2 collective-permute-done.7.three_ref
  20.9 0.5 %collective-permute-start.8 = (f32[8,128]{1,0:T(8,128)S(1)}, f32[8,128]{1,0:T(8,128)S(1)}, u32[]{:S(2)}, u32[]{:S(2)}) collective-permute-start(f32[8,128]{1,0:T(8,128)S(1)} %collective-permute-done.7.three_ref), channel_id=1, source_target_pairs={{0,1},{1,0},{2,3},{3,2},{4,5},{5,4},{6,7},{7,6},{8,9},{9,8},{10,11... | collective-permute-start | bytes 12296 | tf_op jit(solution)/shard_map/ppermute | solution.py:232
  21.4 1.5 %collective-permute-done.6.two_ref = f32[8,128]{1,0:T(8,128)S(1)} collective-permute-done((f32[8,128]{1,0:T(8,128)S(1)}, f32[8,128]{1,0:T(8,128)S(1)}, u32[]{:S(2)}, u32[]{:S(2)}) %collective-permute-start.6) | collective-permute-done | bytes 4128 | tf_op jit(solution)/shard_map/ppermute | solution.py:232
  22.9 0.0 collective-permute-done.8.four_ref
  22.9 0.7 %scale.1 = (f32[64,64]{1,0:T(8,128)}, f32[1,64]{1,0:T(1,128)}) custom-call(f32[128,128]{1,0:T(8,128)S(1)} %get-tuple-element.16.solved_ref, f32[8,128]{1,0:T(8,128)S(1)} %add.11.one_ref, f32[8,128]{1,0:T(8,128)S(1)} %collective-permute-done.6.two_ref, f32[8,128]{1,0:T(8,128)S(1)} %collective-permute-done.7.three_ref, ...), custom_call_target="tpu_custom_call" | custom-call | tf_op jit(solution)/shard_map/scale/pallas_call | solution.py:283
  (6 shorter events, 0.0 us)
Async XLA Ops:
  3.1 3.5 %collective-permute-start = (f32[160,128]{1,0:T(8,128)S(1)}, f32[160,128]{1,0:T(8,128)S(1)}, u32[]{:S(2)}, u32[]{:S(2)}) collective-permute-start(f32[160,128]{1,0:T(8,128)S(1)} %get-tuple-element.14), channel_id=1, source_target_pairs={{0,1},{1,0},{2,3},{3,2},{4,5},{5,4},{6,7},{7,6},{8,9},{9,8},{10,11... | collective-permute-start | bytes 245768 | tf_op jit(solution)/shard_map/ppermute | solution.py:232
  3.2 4.1 %collective-permute-start.3 = (f32[32,128]{1,0:T(8,128)S(1)}, f32[32,128]{1,0:T(8,128)S(1)}, u32[]{:S(2)}, u32[]{:S(2)}) collective-permute-start(f32[32,128]{1,0:T(8,128)S(1)} %get-tuple-element.15.one_ref), channel_id=1, source_target_pairs={{0,3},{1,2},{2,1},{3,0},{4,7},{5,6},{6,5},{7,4},{8,11},{9,10},{10,... | collective-permute-start | bytes 49160 | tf_op jit(solution)/shard_map/ppermute | solution.py:232
  6.6 4.3 %collective-permute-start.1 = (f32[128,128]{1,0:T(8,128)S(1)}, f32[128,128]{1,0:T(8,128)S(1)}, u32[]{:S(2)}, u32[]{:S(2)}) collective-permute-start(f32[128,128]{1,0:T(8,128)S(1)} %slice_add_fusion), channel_id=1, source_target_pairs={{0,3},{1,2},{2,1},{3,0},{4,7},{5,6},{6,5},{7,4},{8,11},{9,10},{10,... | collective-permute-start | bytes 196616 | tf_op jit(solution)/shard_map/ppermute | solution.py:232
  7.3 5.2 %collective-permute-start.4 = (f32[32,128]{1,0:T(8,128)S(1)}, f32[32,128]{1,0:T(8,128)S(1)}, u32[]{:S(2)}, u32[]{:S(2)}) collective-permute-start(f32[32,128]{1,0:T(8,128)S(1)} %added.1.trial_a_ref), channel_id=1, source_target_pairs={{0,5},{1,4},{2,7},{3,6},{4,1},{5,0},{6,3},{7,2},{8,13},{9,12},{10,... | collective-permute-start | bytes 49160 | tf_op jit(solution)/shard_map/ppermute | solution.py:232
  10.9 4.2 %collective-permute-start.2 = (f32[128,128]{1,0:T(8,128)S(1)}, f32[128,128]{1,0:T(8,128)S(1)}, u32[]{:S(2)}, u32[]{:S(2)}) collective-permute-start(f32[128,128]{1,0:T(8,128)S(1)} %add.10.own_ref), channel_id=1, source_target_pairs={{0,5},{1,4},{2,7},{3,6},{4,1},{5,0},{6,3},{7,2},{8,13},{9,12},{10,... | collective-permute-start | bytes 196616 | tf_op jit(solution)/shard_map/ppermute | solution.py:232
  15.3 1.2 %collective-permute-start.5 = (f32[8,128]{1,0:T(8,128)S(1)}, f32[8,128]{1,0:T(8,128)S(1)}, u32[]{:S(2)}, u32[]{:S(2)}) collective-permute-start(f32[8,128]{1,0:T(8,128)S(1)} %get-tuple-element.17), channel_id=1, source_target_pairs={{0,1},{1,0},{2,3},{3,2},{4,5},{5,4},{6,7},{7,6},{8,9},{9,8},{10,11... | collective-permute-start | bytes 12296 | tf_op jit(solution)/shard_map/ppermute | solution.py:232
  16.6 4.3 %collective-permute-start.7 = (f32[8,128]{1,0:T(8,128)S(1)}, f32[8,128]{1,0:T(8,128)S(1)}, u32[]{:S(2)}, u32[]{:S(2)}) collective-permute-start(f32[8,128]{1,0:T(8,128)S(1)} %add.11.one_ref), channel_id=1, source_target_pairs={{0,16},{1,25},{2,18},{3,27},{4,20},{5,29},{6,22},{7,31},{8,24},{9,... | collective-permute-start | bytes 12296 | tf_op jit(solution)/shard_map/ppermute | solution.py:232
  19.9 3.0 %collective-permute-start.6 = (f32[8,128]{1,0:T(8,128)S(1)}, f32[8,128]{1,0:T(8,128)S(1)}, u32[]{:S(2)}, u32[]{:S(2)}) collective-permute-start(f32[8,128]{1,0:T(8,128)S(1)} %add.11.one_ref), channel_id=1, source_target_pairs={{0,9},{1,8},{2,11},{3,10},{4,13},{5,12},{6,15},{7,14},{8,1},{9,0},... | collective-permute-start | bytes 12296 | tf_op jit(solution)/shard_map/ppermute | solution.py:232
  20.9 2.0 %collective-permute-start.8 = (f32[8,128]{1,0:T(8,128)S(1)}, f32[8,128]{1,0:T(8,128)S(1)}, u32[]{:S(2)}, u32[]{:S(2)}) collective-permute-start(f32[8,128]{1,0:T(8,128)S(1)} %collective-permute-done.7.three_ref), channel_id=1, source_target_pairs={{0,1},{1,0},{2,3},{3,2},{4,5},{5,4},{6,7},{7,6},{8,9},{9,8},{10,11... | collective-permute-start | bytes 12296 | tf_op jit(solution)/shard_map/ppermute | solution.py:232

commit v5 on v4

--- a/solution.py
+++ b/solution.py
@@ -79,9 +79,10 @@
     trial = packed(local.astype(jnp.float32))
     left = lax.broadcasted_iota(jnp.int32, (rows, 2 * rank), 1) < rank
     wide = wide_ref[...]
-    for copy in copies[:tri]:
-        copy.wait()
     for t in range(tri):
+        if t % 2 == 0:
+            for copy in copies[t : min(t + 2, tri)]:
+                copy.wait()
         send_ref[t * rows : (t + 1) * rows, :] = row_products(block_ref.at[pl.ds(t * share, share)], wide, trial, left)
     for copy in copies[tri:]:
         copy.wait()
@@ -241,14 +242,17 @@
     got = swap(sent, 0, 0, 1)
     own = own_products(tri, kept, local_factor, wide)
     bin_a, bin_b = sent[held:], got[held:]
+    stages = tri.bit_length() - 1
+
+    def cross(value, stage):
+        return exchange(value, lambda n, t, b: (n, t ^ (1 << (stage + (b ^ parity(t, tri))) % stages), 1 - b))
+
     block = own + got[:held]
-    bit = 1
-    while bit < tri // 2:
-        trial_gram = added(trial_gram, swap(trial_gram, 0, bit, 1))
-        block = block + swap(block, 0, bit, 1)
-        bit *= 2
-    trial_other = swap(trial_gram, 0, bit, 1)
-    other_block = swap(block, 0, bit, 1)
+    for stage in range(stages - 1):
+        trial_gram = added(trial_gram, cross(trial_gram, stage))
+        block = block + cross(block, stage)
+    trial_other = cross(trial_gram, stages - 1)
+    other_block = cross(block, stages - 1)
     inside = pl.BlockSpec(memory_space=pltpu.VMEM)
     inverse = pl.pallas_call(
         inverse_kernel,

time: 23.9 us -> 23.2 us (0.971)
  starting transfers between devices: 11.6 us -> 10.8 us
    ppermute x9, starting transfers between devices: 11.6 us -> 10.8 us  [exchange(): lax.ppermute(value, axes, [(flat(*place), flat(*partner(*place))) for pla...]
where the time goes in v5:
time: 23.2 us; the launch traced here: 23 us
  starting transfers between devices  10.8 us (47%)
  Pallas kernels  5.88 us (25%)
  waiting for transfers between devices  5.63 us (24%)
  between operations  0.66 us (3%)
    ppermute x9, starting transfers between devices, exchange(): lax.ppermute(value, axes, [(flat(*place), flat(*partner(*place))) for pla...  10.8 us
    ppermute x9, waiting for transfers between devices, exchange(): lax.ppermute(value, axes, [(flat(*place), flat(*partner(*place))) for pla...  5.63 us
    pallas_call x1, Pallas kernels, send_products(): pl.pallas_call(functools.partial(send_kernel, tri), in_specs=[outside] *...  2.37 us
    pallas_call x1, Pallas kernels, local(): pl.pallas_call(inverse_kernel, in_specs=[inside] * 4, out_specs=inside, o...  1.74 us
    pallas_call x1, Pallas kernels, own_products(): pl.pallas_call(functools.partial(own_kernel, tri), in_specs=[inside] * 3,...  0.79 us
    pallas_call x1, Pallas kernels, local(): pl.pallas_call(functools.partial(scale_kernel, rows * neur), in_specs=[in...  0.71 us
  transfers between devices with their start and end apart: 9, of which 6 were waited for; matrix products, arithmetic and copies ran while one was open for 0% of the time, Pallas kernels for 11%

profile of v5, /device:TPU:1, one launch (start us, length us, event | category | flops | bytes accessed | tf_op | source)
XLA Modules:
  0.0 23.0 jit_solution(8930489553368808006)
XLA Ops:
  0.6 2.4 %send_products.1 = (f32[160,128]{1,0:T(8,128)S(1)}, f32[32,128]{1,0:T(8,128)S(1)}, bf16[256,32,128]{2,1,0:T(8,128)(2,1)S(1)}, bf16[32,64]{1,0:T(8,128)(2,1)S(1)}, bf16[256,128]{1,0:T(8,128)(2,1)S(1)}) custom-call(bf16[512,32,128]{2,1,0:T(8,128)(2,1)} %tensor_ref.1, bf16[64,128]{1,0:T(8,128)(2,1)} %bitcast.2, bf16[32,64]{1,0:T(8,128)(2,1)} %trial_ref.1), custom_call_target="tpu_custom_call" | custom-call | tf_op jit(solution)/shard_map/send_products/pallas_call | solution.py:108
  3.0 0.1 collective-permute-start
  3.1 2.7 %collective-permute-start.3 = (f32[32,128]{1,0:T(8,128)S(1)}, f32[32,128]{1,0:T(8,128)S(1)}, u32[]{:S(2)}, u32[]{:S(2)}) collective-permute-start(f32[32,128]{1,0:T(8,128)S(1)} %get-tuple-element.15.one_ref), channel_id=1, source_target_pairs={{0,3},{1,4},{2,7},{3,0},{4,1},{5,6},{6,5},{7,2},{8,11},{9,12},{10,... | collective-permute-start | bytes 49160 | tf_op jit(solution)/shard_map/ppermute | solution.py:233
  5.8 0.8 %own_products.1 = f32[128,128]{1,0:T(8,128)S(1)} custom-call(bf16[256,32,128]{2,1,0:T(8,128)(2,1)S(1)} %get-tuple-element.11.held_ref, bf16[32,64]{1,0:T(8,128)(2,1)S(1)} %get-tuple-element.12.local_ref, bf16[256,128]{1,0:T(8,128)(2,1)S(1)} %get-tuple-element.13.wide_ref), custom_call_target="tpu_custom_call" | custom-call | tf_op jit(solution)/shard_map/own_products/pallas_call | solution.py:132
  6.6 0.0 collective-permute-done
  6.6 0.5 %collective-permute-start.1 = (f32[128,128]{1,0:T(8,128)S(1)}, f32[128,128]{1,0:T(8,128)S(1)}, u32[]{:S(2)}, u32[]{:S(2)}) collective-permute-start(f32[128,128]{1,0:T(8,128)S(1)} %slice_add_fusion), channel_id=1, source_target_pairs={{0,3},{1,4},{2,7},{3,0},{4,1},{5,6},{6,5},{7,2},{8,11},{9,12},{10,... | collective-permute-start | bytes 196616 | tf_op jit(solution)/shard_map/ppermute | solution.py:233
  7.0 0.2 collective-permute-done.3.two_ref
  7.2 1.7 %collective-permute-start.4 = (f32[32,128]{1,0:T(8,128)S(1)}, f32[32,128]{1,0:T(8,128)S(1)}, u32[]{:S(2)}, u32[]{:S(2)}) collective-permute-start(f32[32,128]{1,0:T(8,128)S(1)} %added.1.trial_a_ref), channel_id=1, source_target_pairs={{0,5},{1,2},{2,1},{3,6},{4,7},{5,0},{6,3},{7,4},{8,13},{9,10},{10,... | collective-permute-start | bytes 49160 | tf_op jit(solution)/shard_map/ppermute | solution.py:233
  8.9 1.7 %collective-permute-done.1 = f32[128,128]{1,0:T(8,128)S(1)} collective-permute-done((f32[128,128]{1,0:T(8,128)S(1)}, f32[128,128]{1,0:T(8,128)S(1)}, u32[]{:S(2)}, u32[]{:S(2)}) %collective-permute-start.1) | collective-permute-done | bytes 65568 | tf_op jit(solution)/shard_map/ppermute | solution.py:233
  10.6 1.4 %collective-permute-start.2 = (f32[128,128]{1,0:T(8,128)S(1)}, f32[128,128]{1,0:T(8,128)S(1)}, u32[]{:S(2)}, u32[]{:S(2)}) collective-permute-start(f32[128,128]{1,0:T(8,128)S(1)} %add.10.own_ref), channel_id=1, source_target_pairs={{0,5},{1,2},{2,1},{3,6},{4,7},{5,0},{6,3},{7,4},{8,13},{9,10},{10,... | collective-permute-start | bytes 196616 | tf_op jit(solution)/shard_map/ppermute | solution.py:233
  11.9 0.0 collective-permute-done.4.trial_b_ref
  12.0 1.7 %inverse.1.inverse_ref = f32[128,128]{1,0:T(8,128)S(1)} custom-call(f32[32,128]{1,0:T(8,128)S(1)} %slice.10.bin_a_ref, f32[32,128]{1,0:T(8,128)S(1)} %slice.13.bin_b_ref, f32[32,128]{1,0:T(8,128)S(1)} %added.1.trial_a_ref, f32[32,128]{1,0:T(8,128)S(1)} %collective-permute-done.4.trial_b_ref), custom_call_target="tpu_custom_call" | custom-call | flops 10000000000 | bytes 200000 | tf_op jit(solution)/shard_map/inverse/pallas_call | solution.py:257
  13.7 0.7 %collective-permute-done.2.other_ref = f32[128,128]{1,0:T(8,128)S(1)} collective-permute-done((f32[128,128]{1,0:T(8,128)S(1)}, f32[128,128]{1,0:T(8,128)S(1)}, u32[]{:S(2)}, u32[]{:S(2)}) %collective-permute-start.2) | collective-permute-done | bytes 65568 | tf_op jit(solution)/shard_map/ppermute | solution.py:233
  14.3 0.3 %solve.1 = (f32[128,128]{1,0:T(8,128)S(1)}, f32[8,128]{1,0:T(8,128)S(1)}) custom-call(f32[128,128]{1,0:T(8,128)S(1)} %add.10.own_ref, f32[128,128]{1,0:T(8,128)S(1)} %collective-permute-done.2.other_ref, f32[128,128]{1,0:T(8,128)S(1)} %inverse.1.inverse_ref), custom_call_target="tpu_custom_call" | custom-call | tf_op jit(solution)/shard_map/solve/pallas_call | solution.py:265
  14.6 0.2 collective-permute-start.5
  14.8 1.0 %collective-permute-done.5 = f32[8,128]{1,0:T(8,128)S(1)} collective-permute-done((f32[8,128]{1,0:T(8,128)S(1)}, f32[8,128]{1,0:T(8,128)S(1)}, u32[]{:S(2)}, u32[]{:S(2)}) %collective-permute-start.5) | collective-permute-done | bytes 4128 | tf_op jit(solution)/shard_map/ppermute | solution.py:233
  15.8 3.4 %collective-permute-start.7 = (f32[8,128]{1,0:T(8,128)S(1)}, f32[8,128]{1,0:T(8,128)S(1)}, u32[]{:S(2)}, u32[]{:S(2)}) collective-permute-start(f32[8,128]{1,0:T(8,128)S(1)} %add.11.one_ref), channel_id=1, source_target_pairs={{0,16},{1,25},{2,18},{3,27},{4,20},{5,29},{6,22},{7,31},{8,24},{9,... | collective-permute-start | bytes 12296 | tf_op jit(solution)/shard_map/ppermute | solution.py:233
  19.2 0.6 %collective-permute-start.6 = (f32[8,128]{1,0:T(8,128)S(1)}, f32[8,128]{1,0:T(8,128)S(1)}, u32[]{:S(2)}, u32[]{:S(2)}) collective-permute-start(f32[8,128]{1,0:T(8,128)S(1)} %add.11.one_ref), channel_id=1, source_target_pairs={{0,9},{1,8},{2,11},{3,10},{4,13},{5,12},{6,15},{7,14},{8,1},{9,0},... | collective-permute-start | bytes 12296 | tf_op jit(solution)/shard_map/ppermute | solution.py:233
  19.8 0.4 %collective-permute-done.7.three_ref = f32[8,128]{1,0:T(8,128)S(1)} collective-permute-done((f32[8,128]{1,0:T(8,128)S(1)}, f32[8,128]{1,0:T(8,128)S(1)}, u32[]{:S(2)}, u32[]{:S(2)}) %collective-permute-start.7) | collective-permute-done | bytes 4128 | tf_op jit(solution)/shard_map/ppermute | solution.py:233
  20.2 0.2 %collective-permute-start.8 = (f32[8,128]{1,0:T(8,128)S(1)}, f32[8,128]{1,0:T(8,128)S(1)}, u32[]{:S(2)}, u32[]{:S(2)}) collective-permute-start(f32[8,128]{1,0:T(8,128)S(1)} %collective-permute-done.7.three_ref), channel_id=1, source_target_pairs={{0,1},{1,0},{2,3},{3,2},{4,5},{5,4},{6,7},{7,6},{8,9},{9,8},{10,11... | collective-permute-start | bytes 12296 | tf_op jit(solution)/shard_map/ppermute | solution.py:233
  20.5 1.8 %collective-permute-done.6.two_ref = f32[8,128]{1,0:T(8,128)S(1)} collective-permute-done((f32[8,128]{1,0:T(8,128)S(1)}, f32[8,128]{1,0:T(8,128)S(1)}, u32[]{:S(2)}, u32[]{:S(2)}) %collective-permute-start.6) | collective-permute-done | bytes 4128 | tf_op jit(solution)/shard_map/ppermute | solution.py:233
  22.3 0.0 collective-permute-done.8.four_ref
  22.3 0.7 %scale.1 = (f32[64,64]{1,0:T(8,128)}, f32[1,64]{1,0:T(1,128)}) custom-call(f32[128,128]{1,0:T(8,128)S(1)} %get-tuple-element.16.solved_ref, f32[8,128]{1,0:T(8,128)S(1)} %add.11.one_ref, f32[8,128]{1,0:T(8,128)S(1)} %collective-permute-done.6.two_ref, f32[8,128]{1,0:T(8,128)S(1)} %collective-permute-done.7.three_ref, ...), custom_call_target="tpu_custom_call" | custom-call | tf_op jit(solution)/shard_map/scale/pallas_call | solution.py:287
  (6 shorter events, 0.0 us)
Async XLA Ops:
  3.0 3.6 %collective-permute-start = (f32[160,128]{1,0:T(8,128)S(1)}, f32[160,128]{1,0:T(8,128)S(1)}, u32[]{:S(2)}, u32[]{:S(2)}) collective-permute-start(f32[160,128]{1,0:T(8,128)S(1)} %get-tuple-element.14), channel_id=1, source_target_pairs={{0,1},{1,0},{2,3},{3,2},{4,5},{5,4},{6,7},{7,6},{8,9},{9,8},{10,11... | collective-permute-start | bytes 245768 | tf_op jit(solution)/shard_map/ppermute | solution.py:233
  3.1 4.1 %collective-permute-start.3 = (f32[32,128]{1,0:T(8,128)S(1)}, f32[32,128]{1,0:T(8,128)S(1)}, u32[]{:S(2)}, u32[]{:S(2)}) collective-permute-start(f32[32,128]{1,0:T(8,128)S(1)} %get-tuple-element.15.one_ref), channel_id=1, source_target_pairs={{0,3},{1,4},{2,7},{3,0},{4,1},{5,6},{6,5},{7,2},{8,11},{9,12},{10,... | collective-permute-start | bytes 49160 | tf_op jit(solution)/shard_map/ppermute | solution.py:233
  6.6 4.0 %collective-permute-start.1 = (f32[128,128]{1,0:T(8,128)S(1)}, f32[128,128]{1,0:T(8,128)S(1)}, u32[]{:S(2)}, u32[]{:S(2)}) collective-permute-start(f32[128,128]{1,0:T(8,128)S(1)} %slice_add_fusion), channel_id=1, source_target_pairs={{0,3},{1,4},{2,7},{3,0},{4,1},{5,6},{6,5},{7,2},{8,11},{9,12},{10,... | collective-permute-start | bytes 196616 | tf_op jit(solution)/shard_map/ppermute | solution.py:233
  7.2 4.7 %collective-permute-start.4 = (f32[32,128]{1,0:T(8,128)S(1)}, f32[32,128]{1,0:T(8,128)S(1)}, u32[]{:S(2)}, u32[]{:S(2)}) collective-permute-start(f32[32,128]{1,0:T(8,128)S(1)} %added.1.trial_a_ref), channel_id=1, source_target_pairs={{0,5},{1,2},{2,1},{3,6},{4,7},{5,0},{6,3},{7,4},{8,13},{9,10},{10,... | collective-permute-start | bytes 49160 | tf_op jit(solution)/shard_map/ppermute | solution.py:233
  10.6 3.8 %collective-permute-start.2 = (f32[128,128]{1,0:T(8,128)S(1)}, f32[128,128]{1,0:T(8,128)S(1)}, u32[]{:S(2)}, u32[]{:S(2)}) collective-permute-start(f32[128,128]{1,0:T(8,128)S(1)} %add.10.own_ref), channel_id=1, source_target_pairs={{0,5},{1,2},{2,1},{3,6},{4,7},{5,0},{6,3},{7,4},{8,13},{9,10},{10,... | collective-permute-start | bytes 196616 | tf_op jit(solution)/shard_map/ppermute | solution.py:233
  14.6 1.2 %collective-permute-start.5 = (f32[8,128]{1,0:T(8,128)S(1)}, f32[8,128]{1,0:T(8,128)S(1)}, u32[]{:S(2)}, u32[]{:S(2)}) collective-permute-start(f32[8,128]{1,0:T(8,128)S(1)} %get-tuple-element.17), channel_id=1, source_target_pairs={{0,1},{1,0},{2,3},{3,2},{4,5},{5,4},{6,7},{7,6},{8,9},{9,8},{10,11... | collective-permute-start | bytes 12296 | tf_op jit(solution)/shard_map/ppermute | solution.py:233
  15.8 4.4 %collective-permute-start.7 = (f32[8,128]{1,0:T(8,128)S(1)}, f32[8,128]{1,0:T(8,128)S(1)}, u32[]{:S(2)}, u32[]{:S(2)}) collective-permute-start(f32[8,128]{1,0:T(8,128)S(1)} %add.11.one_ref), channel_id=1, source_target_pairs={{0,16},{1,25},{2,18},{3,27},{4,20},{5,29},{6,22},{7,31},{8,24},{9,... | collective-permute-start | bytes 12296 | tf_op jit(solution)/shard_map/ppermute | solution.py:233
  19.2 3.0 %collective-permute-start.6 = (f32[8,128]{1,0:T(8,128)S(1)}, f32[8,128]{1,0:T(8,128)S(1)}, u32[]{:S(2)}, u32[]{:S(2)}) collective-permute-start(f32[8,128]{1,0:T(8,128)S(1)} %add.11.one_ref), channel_id=1, source_target_pairs={{0,9},{1,8},{2,11},{3,10},{4,13},{5,12},{6,15},{7,14},{8,1},{9,0},... | collective-permute-start | bytes 12296 | tf_op jit(solution)/shard_map/ppermute | solution.py:233
  20.2 2.0 %collective-permute-start.8 = (f32[8,128]{1,0:T(8,128)S(1)}, f32[8,128]{1,0:T(8,128)S(1)}, u32[]{:S(2)}, u32[]{:S(2)}) collective-permute-start(f32[8,128]{1,0:T(8,128)S(1)} %collective-permute-done.7.three_ref), channel_id=1, source_target_pairs={{0,1},{1,0},{2,3},{3,2},{4,5},{5,4},{6,7},{7,6},{8,9},{9,8},{10,11... | collective-permute-start | bytes 12296 | tf_op jit(solution)/shard_map/ppermute | solution.py:233

commit v6 on v5

--- a/solution.py
+++ b/solution.py
@@ -32,17 +32,24 @@
     return jnp.concatenate([value[:count], value[count:]], axis=1)
 
 
-def row_products(part, wide, trial, left):
+def sections(part, wide):
     share, trials, bins = part.shape
     pair = trials // 2
-    rank = wide.shape[1] // 2
-    rows = share // 2
     low = part[:, :pair, :].reshape(share * pair, bins)
     high = part[:, pair:, :].reshape(share * pair, bins)
     section = jnp.dot(jnp.concatenate([low, high], axis=1), wide, preferred_element_type=jnp.float32)
-    total = jnp.sum(section.reshape(share, pair, 2 * rank) * trial[None], axis=1)
-    total = total + pltpu.roll(total, rank, 1)
+    return section.reshape(share, pair, wide.shape[1])
+
+
+def over_trials(section, trial, left):
+    rows = section.shape[0] // 2
+    total = jnp.sum(section * trial[None], axis=1)
+    total = total + pltpu.roll(total, trial.shape[1] // 2, 1)
     return jnp.where(left, total[:rows], total[rows:])
+
+
+def row_products(part, wide, trial, left):
+    return over_trials(sections(part, wide), trial, left)
 
 
 def send_kernel(tri, tensor_ref, bin_t_ref, trial_ref, send_ref, gram_ref, held_ref, local_ref, wide_ref, block_ref, bin_ref, sems):
@@ -79,11 +86,14 @@
     trial = packed(local.astype(jnp.float32))
     left = lax.broadcasted_iota(jnp.int32, (rows, 2 * rank), 1) < rank
     wide = wide_ref[...]
-    for t in range(tri):
-        if t % 2 == 0:
-            for copy in copies[t : min(t + 2, tri)]:
-                copy.wait()
-        send_ref[t * rows : (t + 1) * rows, :] = row_products(block_ref.at[pl.ds(t * share, share)], wide, trial, left)
+    for copy in copies[: tri // 2]:
+        copy.wait()
+    early = [sections(block_ref.at[pl.ds(t * share, share)], wide) for t in range(tri // 2)]
+    for copy in copies[tri // 2 : tri]:
+        copy.wait()
+    late = [sections(block_ref.at[pl.ds(t * share, share)], wide) for t in range(tri // 2, tri)]
+    for t, section in enumerate(early + late):
+        send_ref[t * rows : (t + 1) * rows, :] = over_trials(section, trial, left)
     for copy in copies[tri:]:
         copy.wait()
 
@@ -243,6 +253,7 @@
     own = own_products(tri, kept, local_factor, wide)
     bin_a, bin_b = sent[held:], got[held:]
     stages = tri.bit_length() - 1
+    trial_gram, own = lax.optimization_barrier((trial_gram, own))
 
     def cross(value, stage):
         return exchange(value, lambda n, t, b: (n, t ^ (1 << (stage + (b ^ parity(t, tri))) % stages), 1 - b))
@@ -266,7 +277,7 @@
         solve_kernel,
         in_specs=[inside] * 3,
         out_specs=(inside, inside),
-        out_shape=(pltpu.VMEM((held, 2 * rank), f32), pltpu.VMEM((SUB, 2 * rank), f32)),
+        out_shape=(pltpu.VMEM((held, 2 * rank), f32), pltpu.VMEM((1, 2 * rank), f32)),
         name="solve",
     )(*held_in(block, other_block, inverse))
     squares = squares + swap(squares, 0, 0, 1)

time: 23.2 us -> 22.8 us (0.983)
  waiting for transfers between devices: 5.63 us -> 4.61 us
  starting transfers between devices: 10.8 us -> 11.4 us
    ppermute x9, waiting for transfers between devices: 5.63 us -> 4.61 us  [exchange(): lax.ppermute(value, axes, [(flat(*place), flat(*partner(*place))) for pla...]
    ppermute x9, starting transfers between devices: 10.8 us -> 11.4 us  [exchange(): lax.ppermute(value, axes, [(flat(*place), flat(*partner(*place))) for pla...]
where the time goes in v6:
time: 22.8 us; the launch traced here: 22.6 us
  starting transfers between devices  11.4 us (50%)
  Pallas kernels  5.85 us (26%)
  waiting for transfers between devices  4.61 us (20%)
  between operations  0.66 us (3%)
    ppermute x9, starting transfers between devices, exchange(): lax.ppermute(value, axes, [(flat(*place), flat(*partner(*place))) for pla...  11.4 us
    ppermute x9, waiting for transfers between devices, exchange(): lax.ppermute(value, axes, [(flat(*place), flat(*partner(*place))) for pla...  4.61 us
    pallas_call x1, Pallas kernels, send_products(): pl.pallas_call(functools.partial(send_kernel, tri), in_specs=[outside] *...  2.33 us
    pallas_call x1, Pallas kernels, local(): pl.pallas_call(inverse_kernel, in_specs=[inside] * 4, out_specs=inside, o...  1.74 us
    pallas_call x1, Pallas kernels, own_products(): pl.pallas_call(functools.partial(own_kernel, tri), in_specs=[inside] * 3,...  0.79 us
    pallas_call x1, Pallas kernels, local(): pl.pallas_call(functools.partial(scale_kernel, rows * neur), in_specs=[in...  0.71 us
  transfers between devices with their start and end apart: 9, of which 6 were waited for; matrix products, arithmetic and copies ran while one was open for 0% of the time, Pallas kernels for 11%

profile of v6, /device:TPU:1, one launch (start us, length us, event | category | flops | bytes accessed | tf_op | source)
XLA Modules:
  0.0 22.6 jit_solution(10642186887243752005)
XLA Ops:
  0.6 2.3 %send_products.1 = (f32[160,128]{1,0:T(8,128)S(1)}, f32[32,128]{1,0:T(8,128)S(1)}, bf16[256,32,128]{2,1,0:T(8,128)(2,1)S(1)}, bf16[32,64]{1,0:T(8,128)(2,1)S(1)}, bf16[256,128]{1,0:T(8,128)(2,1)S(1)}) custom-call(bf16[512,32,128]{2,1,0:T(8,128)(2,1)} %tensor_ref.1, bf16[64,128]{1,0:T(8,128)(2,1)} %bitcast.2, bf16[32,64]{1,0:T(8,128)(2,1)} %trial_ref.1), custom_call_target="tpu_custom_call" | custom-call | tf_op jit(solution)/shard_map/send_products/pallas_call | solution.py:118
  3.0 0.1 collective-permute-start
  3.1 0.8 %own_products.1 = f32[128,128]{1,0:T(8,128)S(1)} custom-call(bf16[256,32,128]{2,1,0:T(8,128)(2,1)S(1)} %get-tuple-element.14.held_ref, bf16[32,64]{1,0:T(8,128)(2,1)S(1)} %get-tuple-element.15.local_ref, bf16[256,128]{1,0:T(8,128)(2,1)S(1)} %get-tuple-element.16.wide_ref), custom_call_target="tpu_custom_call" | custom-call | tf_op jit(solution)/shard_map/own_products/pallas_call | solution.py:142
  3.9 2.6 %collective-permute-start.3 = (f32[32,128]{1,0:T(8,128)S(1)}, f32[32,128]{1,0:T(8,128)S(1)}, u32[]{:S(2)}, u32[]{:S(2)}) collective-permute-start(f32[32,128]{1,0:T(8,128)S(1)} %get-tuple-element.19.one_ref), channel_id=1, source_target_pairs={{0,3},{1,4},{2,7},{3,0},{4,1},{5,6},{6,5},{7,2},{8,11},{9,12},{10,... | collective-permute-start | bytes 49160 | tf_op jit(solution)/shard_map/ppermute | solution.py:243
  6.5 0.0 collective-permute-done
  6.5 0.5 %collective-permute-start.1 = (f32[128,128]{1,0:T(8,128)S(1)}, f32[128,128]{1,0:T(8,128)S(1)}, u32[]{:S(2)}, u32[]{:S(2)}) collective-permute-start(f32[128,128]{1,0:T(8,128)S(1)} %slice_add_fusion), channel_id=1, source_target_pairs={{0,3},{1,4},{2,7},{3,0},{4,1},{5,6},{6,5},{7,2},{8,11},{9,12},{10,... | collective-permute-start | bytes 196616 | tf_op jit(solution)/shard_map/ppermute | solution.py:243
  7.0 0.9 %collective-permute-done.3.two_ref = f32[32,128]{1,0:T(8,128)S(1)} collective-permute-done((f32[32,128]{1,0:T(8,128)S(1)}, f32[32,128]{1,0:T(8,128)S(1)}, u32[]{:S(2)}, u32[]{:S(2)}) %collective-permute-start.3) | collective-permute-done | bytes 16416 | tf_op jit(solution)/shard_map/ppermute | solution.py:243
  8.0 1.6 %collective-permute-start.4 = (f32[32,128]{1,0:T(8,128)S(1)}, f32[32,128]{1,0:T(8,128)S(1)}, u32[]{:S(2)}, u32[]{:S(2)}) collective-permute-start(f32[32,128]{1,0:T(8,128)S(1)} %added.1.trial_a_ref), channel_id=1, source_target_pairs={{0,5},{1,2},{2,1},{3,6},{4,7},{5,0},{6,3},{7,4},{8,13},{9,10},{10,... | collective-permute-start | bytes 49160 | tf_op jit(solution)/shard_map/ppermute | solution.py:243
  9.6 0.7 %collective-permute-done.1 = f32[128,128]{1,0:T(8,128)S(1)} collective-permute-done((f32[128,128]{1,0:T(8,128)S(1)}, f32[128,128]{1,0:T(8,128)S(1)}, u32[]{:S(2)}, u32[]{:S(2)}) %collective-permute-start.1) | collective-permute-done | bytes 65568 | tf_op jit(solution)/shard_map/ppermute | solution.py:243
  10.3 1.6 %collective-permute-start.2 = (f32[128,128]{1,0:T(8,128)S(1)}, f32[128,128]{1,0:T(8,128)S(1)}, u32[]{:S(2)}, u32[]{:S(2)}) collective-permute-start(f32[128,128]{1,0:T(8,128)S(1)} %add.10.own_ref), channel_id=1, source_target_pairs={{0,5},{1,2},{2,1},{3,6},{4,7},{5,0},{6,3},{7,4},{8,13},{9,10},{10,... | collective-permute-start | bytes 196616 | tf_op jit(solution)/shard_map/ppermute | solution.py:243
  11.9 0.0 collective-permute-done.4.trial_b_ref
  11.9 1.7 %inverse.1.inverse_ref = f32[128,128]{1,0:T(8,128)S(1)} custom-call(f32[32,128]{1,0:T(8,128)S(1)} %slice.10.bin_a_ref, f32[32,128]{1,0:T(8,128)S(1)} %slice.13.bin_b_ref, f32[32,128]{1,0:T(8,128)S(1)} %added.1.trial_a_ref, f32[32,128]{1,0:T(8,128)S(1)} %collective-permute-done.4.trial_b_ref), custom_call_target="tpu_custom_call" | custom-call | flops 10000000000 | bytes 200000 | tf_op jit(solution)/shard_map/inverse/pallas_call | solution.py:268
  13.7 0.4 %collective-permute-done.2.other_ref = f32[128,128]{1,0:T(8,128)S(1)} collective-permute-done((f32[128,128]{1,0:T(8,128)S(1)}, f32[128,128]{1,0:T(8,128)S(1)}, u32[]{:S(2)}, u32[]{:S(2)}) %collective-permute-start.2) | collective-permute-done | bytes 65568 | tf_op jit(solution)/shard_map/ppermute | solution.py:243
  14.1 0.3 %solve.1 = (f32[128,128]{1,0:T(8,128)S(1)}, f32[1,128]{1,0:T(1,128)S(1)}) custom-call(f32[128,128]{1,0:T(8,128)S(1)} %add.10.own_ref, f32[128,128]{1,0:T(8,128)S(1)} %collective-permute-done.2.other_ref, f32[128,128]{1,0:T(8,128)S(1)} %inverse.1.inverse_ref), custom_call_target="tpu_custom_call" | custom-call | tf_op jit(solution)/shard_map/solve/pallas_call | solution.py:276
  14.4 0.4 %collective-permute-start.5 = (f32[1,128]{1,0:T(1,128)S(1)}, f32[1,128]{1,0:T(1,128)S(1)}, u32[]{:S(2)}, u32[]{:S(2)}) collective-permute-start(f32[1,128]{1,0:T(1,128)S(1)} %get-tuple-element.21), channel_id=1, source_target_pairs={{0,1},{1,0},{2,3},{3,2},{4,5},{5,4},{6,7},{7,6},{8,9},{9,8},{10,11... | collective-permute-start | bytes 1544 | tf_op jit(solution)/shard_map/ppermute | solution.py:243
  14.8 0.8 %collective-permute-done.5 = f32[1,128]{1,0:T(1,128)S(1)} collective-permute-done((f32[1,128]{1,0:T(1,128)S(1)}, f32[1,128]{1,0:T(1,128)S(1)}, u32[]{:S(2)}, u32[]{:S(2)}) %collective-permute-start.5) | collective-permute-done | bytes 544 | tf_op jit(solution)/shard_map/ppermute | solution.py:243
  15.6 3.3 %collective-permute-start.7 = (f32[1,128]{1,0:T(1,128)S(1)}, f32[1,128]{1,0:T(1,128)S(1)}, u32[]{:S(2)}, u32[]{:S(2)}) collective-permute-start(f32[1,128]{1,0:T(1,128)S(1)} %add.11.one_ref), channel_id=1, source_target_pairs={{0,16},{1,25},{2,18},{3,27},{4,20},{5,29},{6,22},{7,31},{8,24},{9,... | collective-permute-start | bytes 1544 | tf_op jit(solution)/shard_map/ppermute | solution.py:243
  18.9 0.8 %collective-permute-start.6 = (f32[1,128]{1,0:T(1,128)S(1)}, f32[1,128]{1,0:T(1,128)S(1)}, u32[]{:S(2)}, u32[]{:S(2)}) collective-permute-start(f32[1,128]{1,0:T(1,128)S(1)} %add.11.one_ref), channel_id=1, source_target_pairs={{0,9},{1,8},{2,11},{3,10},{4,13},{5,12},{6,15},{7,14},{8,1},{9,0},... | collective-permute-start | bytes 1544 | tf_op jit(solution)/shard_map/ppermute | solution.py:243
  19.7 0.2 collective-permute-done.7.three_ref
  19.8 0.5 %collective-permute-start.8 = (f32[1,128]{1,0:T(1,128)S(1)}, f32[1,128]{1,0:T(1,128)S(1)}, u32[]{:S(2)}, u32[]{:S(2)}) collective-permute-start(f32[1,128]{1,0:T(1,128)S(1)} %collective-permute-done.7.three_ref), channel_id=1, source_target_pairs={{0,1},{1,0},{2,3},{3,2},{4,5},{5,4},{6,7},{7,6},{8,9},{9,8},{10,11... | collective-permute-start | bytes 1544 | tf_op jit(solution)/shard_map/ppermute | solution.py:243
  20.3 1.5 %collective-permute-done.6.two_ref = f32[1,128]{1,0:T(1,128)S(1)} collective-permute-done((f32[1,128]{1,0:T(1,128)S(1)}, f32[1,128]{1,0:T(1,128)S(1)}, u32[]{:S(2)}, u32[]{:S(2)}) %collective-permute-start.6) | collective-permute-done | bytes 544 | tf_op jit(solution)/shard_map/ppermute | solution.py:243
  21.9 0.0 collective-permute-done.8.four_ref
  21.9 0.7 %scale.1 = (f32[64,64]{1,0:T(8,128)}, f32[1,64]{1,0:T(1,128)}) custom-call(f32[128,128]{1,0:T(8,128)S(1)} %get-tuple-element.20.solved_ref, f32[1,128]{1,0:T(1,128)S(1)} %add.11.one_ref, f32[1,128]{1,0:T(1,128)S(1)} %collective-permute-done.6.two_ref, f32[1,128]{1,0:T(1,128)S(1)} %collective-permute-done.7.three_ref, ...), custom_call_target="tpu_custom_call" | custom-call | tf_op jit(solution)/shard_map/scale/pallas_call | solution.py:298
  (6 shorter events, 0.0 us)
Async XLA Ops:
  3.0 3.5 %collective-permute-start = (f32[160,128]{1,0:T(8,128)S(1)}, f32[160,128]{1,0:T(8,128)S(1)}, u32[]{:S(2)}, u32[]{:S(2)}) collective-permute-start(f32[160,128]{1,0:T(8,128)S(1)} %get-tuple-element.18), channel_id=1, source_target_pairs={{0,1},{1,0},{2,3},{3,2},{4,5},{5,4},{6,7},{7,6},{8,9},{9,8},{10,11... | collective-permute-start | bytes 245768 | tf_op jit(solution)/shard_map/ppermute | solution.py:243
  3.9 4.1 %collective-permute-start.3 = (f32[32,128]{1,0:T(8,128)S(1)}, f32[32,128]{1,0:T(8,128)S(1)}, u32[]{:S(2)}, u32[]{:S(2)}) collective-permute-start(f32[32,128]{1,0:T(8,128)S(1)} %get-tuple-element.19.one_ref), channel_id=1, source_target_pairs={{0,3},{1,4},{2,7},{3,0},{4,1},{5,6},{6,5},{7,2},{8,11},{9,12},{10,... | collective-permute-start | bytes 49160 | tf_op jit(solution)/shard_map/ppermute | solution.py:243
  6.5 3.8 %collective-permute-start.1 = (f32[128,128]{1,0:T(8,128)S(1)}, f32[128,128]{1,0:T(8,128)S(1)}, u32[]{:S(2)}, u32[]{:S(2)}) collective-permute-start(f32[128,128]{1,0:T(8,128)S(1)} %slice_add_fusion), channel_id=1, source_target_pairs={{0,3},{1,4},{2,7},{3,0},{4,1},{5,6},{6,5},{7,2},{8,11},{9,12},{10,... | collective-permute-start | bytes 196616 | tf_op jit(solution)/shard_map/ppermute | solution.py:243
  8.0 4.0 %collective-permute-start.4 = (f32[32,128]{1,0:T(8,128)S(1)}, f32[32,128]{1,0:T(8,128)S(1)}, u32[]{:S(2)}, u32[]{:S(2)}) collective-permute-start(f32[32,128]{1,0:T(8,128)S(1)} %added.1.trial_a_ref), channel_id=1, source_target_pairs={{0,5},{1,2},{2,1},{3,6},{4,7},{5,0},{6,3},{7,4},{8,13},{9,10},{10,... | collective-permute-start | bytes 49160 | tf_op jit(solution)/shard_map/ppermute | solution.py:243
  10.3 3.8 %collective-permute-start.2 = (f32[128,128]{1,0:T(8,128)S(1)}, f32[128,128]{1,0:T(8,128)S(1)}, u32[]{:S(2)}, u32[]{:S(2)}) collective-permute-start(f32[128,128]{1,0:T(8,128)S(1)} %add.10.own_ref), channel_id=1, source_target_pairs={{0,5},{1,2},{2,1},{3,6},{4,7},{5,0},{6,3},{7,4},{8,13},{9,10},{10,... | collective-permute-start | bytes 196616 | tf_op jit(solution)/shard_map/ppermute | solution.py:243
  14.4 1.2 %collective-permute-start.5 = (f32[1,128]{1,0:T(1,128)S(1)}, f32[1,128]{1,0:T(1,128)S(1)}, u32[]{:S(2)}, u32[]{:S(2)}) collective-permute-start(f32[1,128]{1,0:T(1,128)S(1)} %get-tuple-element.21), channel_id=1, source_target_pairs={{0,1},{1,0},{2,3},{3,2},{4,5},{5,4},{6,7},{7,6},{8,9},{9,8},{10,11... | collective-permute-start | bytes 1544 | tf_op jit(solution)/shard_map/ppermute | solution.py:243
  15.6 4.2 %collective-permute-start.7 = (f32[1,128]{1,0:T(1,128)S(1)}, f32[1,128]{1,0:T(1,128)S(1)}, u32[]{:S(2)}, u32[]{:S(2)}) collective-permute-start(f32[1,128]{1,0:T(1,128)S(1)} %add.11.one_ref), channel_id=1, source_target_pairs={{0,16},{1,25},{2,18},{3,27},{4,20},{5,29},{6,22},{7,31},{8,24},{9,... | collective-permute-start | bytes 1544 | tf_op jit(solution)/shard_map/ppermute | solution.py:243
  18.9 3.0 %collective-permute-start.6 = (f32[1,128]{1,0:T(1,128)S(1)}, f32[1,128]{1,0:T(1,128)S(1)}, u32[]{:S(2)}, u32[]{:S(2)}) collective-permute-start(f32[1,128]{1,0:T(1,128)S(1)} %add.11.one_ref), channel_id=1, source_target_pairs={{0,9},{1,8},{2,11},{3,10},{4,13},{5,12},{6,15},{7,14},{8,1},{9,0},... | collective-permute-start | bytes 1544 | tf_op jit(solution)/shard_map/ppermute | solution.py:243
  19.8 2.0 %collective-permute-start.8 = (f32[1,128]{1,0:T(1,128)S(1)}, f32[1,128]{1,0:T(1,128)S(1)}, u32[]{:S(2)}, u32[]{:S(2)}) collective-permute-start(f32[1,128]{1,0:T(1,128)S(1)} %collective-permute-done.7.three_ref), channel_id=1, source_target_pairs={{0,1},{1,0},{2,3},{3,2},{4,5},{5,4},{6,7},{7,6},{8,9},{9,8},{10,11... | collective-permute-start | bytes 1544 | tf_op jit(solution)/shard_map/ppermute | solution.py:243
